TPU v7x, 32 devices: a whole 2x2x4 slice. The times are simulated.
32 devices in a mesh: grp: 2 (over x), own: 8 (over z, y), shot: 2 (over core).
Axes of the slice: x: 2, y: 2, z: 4, core: 2. Of those that a mesh axis runs over, the one named last changes fastest.
Arguments:
- velocity: bfloat16 [2048, 4, 4, 128], P(('grp', 'own')), parts along dimension 0, may hold values from 1.5 to 4.5
- density: bfloat16 [2048, 4, 4, 128], P(('grp', 'own')), parts along dimension 0, may hold values from 1 to 2.59375
- tile_home: int32 [2048], P('grp'), parts along dimension 0, may hold values from 0 to 1023, as said below
- footprints: int32 [16, 2, 2, 64], P('grp'), parts along dimension 0, may hold values from 0 to 1023, as said below
- source_cell: int32 [16, 2, 2], P(('grp', 'own'), 'shot'), parts along dimension 0, may hold values from 0 to 131071
- source_wave: float32 [16, 2, 2, 2], P(('grp', 'own'), 'shot'), parts along dimension 0, may hold values from -16 to 16
- receivers: int32 [16, 2, 2, 128], P(('grp', 'own'), 'shot'), parts along dimension 0, may hold values from 0 to 131071
- observed: float32 [16, 2, 2, 2, 128], P(('grp', 'own'), 'shot'), parts along dimension 0, may hold values from -6 to 6
- pressure_old: bfloat16 [16, 2, 2, 32, 32, 128], P(('grp', 'own'), 'shot'), parts along dimension 0, may hold values from -6 to 6
- pressure_now: bfloat16 [16, 2, 2, 32, 32, 128], P(('grp', 'own'), 'shot'), parts along dimension 0, may hold values from -6 to 6
- adjoint_next: bfloat16 [16, 2, 2, 32, 32, 128], P(('grp', 'own'), 'shot'), parts along dimension 0, may hold values from -6 to 6
- adjoint_now: bfloat16 [16, 2, 2, 32, 32, 128], P(('grp', 'own'), 'shot'), parts along dimension 0, may hold values from -6 to 6
Outputs:
- velocity_gradient: float32 [2048, 4, 4, 128], P(('grp', 'own'), 'shot'), parts along dimension 0
There are 2 independent parts, one for each index of `grp`. A program takes and returns all parts, laid end to end along the dimension named above; each array names one. Nothing has to cross between parts.
Inputs may be any that keep to these rules, and one draw needn't show every extreme that they name: `tile_home`: a permutation of the rows; a row's owner is row // 128; with tiles numbered row by row over the 32 x 32 grid, every square block of 8 x 8 tiles holds exactly 8 tiles of each owner. `footprints`: each list names the tiles of one square block of 8 x 8 tiles of the grid, row by row.
All inputs are finite; a program needn't handle non-finite values.
Results may differ from a plain program's by a relative error of at most 0.0003.
Values may be sent and summed in bfloat16 or wider, within the bound.
A program may use at most 64 MiB of HBM per device.

v0:
```python
import jax
import jax.numpy as jnp
from jax import lax
from jax.sharding import PartitionSpec as P

FT = 8


STENCIL = (1225.0 / 1024.0, -245.0 / 3072.0, 49.0 / 5120.0, -5.0 / 7168.0)
COURANT = 0.09


def take_cells(wavefield, dimension, first_cell, length):
    return lax.slice_in_dim(wavefield, first_cell, first_cell + length, axis=dimension)


def half_buoyancy(buoyancy, dimension):
    length = buoyancy.shape[dimension]
    following = jnp.concatenate(
        [
            take_cells(buoyancy, dimension, 1, length - 1),
            take_cells(buoyancy, dimension, length - 1, 1),
        ],
        axis=dimension,
    )
    return 0.5 * (buoyancy + following)


def pad_along(wavefield, dimension):
    widths = [(4, 4) if index_dim == dimension else (0, 0) for index_dim in range(3)]
    return jnp.pad(wavefield, widths)


def apply_operator(wavefield, half_buoys):
    summed = jnp.zeros_like(wavefield)
    for dimension in range(3):
        length = wavefield.shape[dimension]
        padded = pad_along(wavefield, dimension)
        gradient = jnp.zeros_like(wavefield)
        for position, weight in enumerate(STENCIL):
            distance = position + 1
            gradient = gradient + weight * (
                take_cells(padded, dimension, 4 + distance, length)
                - take_cells(padded, dimension, 5 - distance, length)
            )
        flux_pad = pad_along(half_buoys[dimension] * gradient, dimension)
        for position, weight in enumerate(STENCIL):
            distance = position + 1
            summed = summed + weight * (
                take_cells(flux_pad, dimension, 3 + distance, length)
                - take_cells(flux_pad, dimension, 4 - distance, length)
            )
    return summed


def inject(wavefield, cell_index, amounts):
    return wavefield.reshape(-1).at[cell_index].add(amounts).reshape(wavefield.shape)


def record(wavefield, cell_index):
    return wavefield.reshape(-1)[cell_index]


def run_shot(
    velocity,
    density,
    pressure_old,
    pressure_now,
    adjoint_next,
    adjoint_now,
    source_cell,
    source_wave,
    receivers,
    observed,
):
    coupling = (COURANT * velocity) ** 2 * density
    buoyancy = 1.0 / density
    half_buoys = tuple((half_buoyancy(buoyancy, dimension) for dimension in range(3)))
    image_one = apply_operator(pressure_now, half_buoys)
    pressure_two = inject(
        2.0 * pressure_now - pressure_old + coupling * image_one, source_cell, source_wave[0]
    )
    image_two = apply_operator(pressure_two, half_buoys)
    pressure_three = inject(
        2.0 * pressure_two - pressure_now + coupling * image_two, source_cell, source_wave[1]
    )
    misfit_one = record(pressure_two, receivers) - observed[0]
    misfit_two = record(pressure_three, receivers) - observed[1]
    adjoint_one = inject(
        2.0 * adjoint_now - adjoint_next + coupling * apply_operator(adjoint_now, half_buoys),
        receivers,
        misfit_two,
    )
    adjoint_zero = inject(
        2.0 * adjoint_one - adjoint_now + coupling * apply_operator(adjoint_one, half_buoys),
        receivers,
        misfit_one,
    )
    return (
        2.0
        * COURANT
        * COURANT
        * velocity
        * density
        * (adjoint_one * image_two + adjoint_zero * image_one)
    )


def tiles_to_field(tiles, per_side):
    tile_x, tile_y, depth = (tiles.shape[1], tiles.shape[2], tiles.shape[3])
    grid = tiles.reshape(per_side, per_side, tile_x, tile_y, depth).transpose(0, 2, 1, 3, 4)
    return grid.reshape(per_side * tile_x, per_side * tile_y, depth)


def field_to_tiles(wavefield, per_side):
    tile_x = wavefield.shape[0] // per_side
    tile_y = wavefield.shape[1] // per_side
    depth = wavefield.shape[2]
    grid = wavefield.reshape(per_side, tile_x, per_side, tile_y, depth).transpose(0, 2, 1, 3, 4)
    return grid.reshape(per_side * per_side, tile_x, tile_y, depth)


def place_rows(row_index, arrived, tiles_held):
    selector = (row_index[None, :] == jnp.arange(tiles_held)[:, None]).astype(jnp.float32)
    flat_rows = arrived.reshape(row_index.shape[0], -1)
    placed = jnp.dot(
        selector, flat_rows, precision=lax.Precision.HIGHEST, preferred_element_type=jnp.float32
    )
    return placed.reshape((tiles_held,) + arrived.shape[1:])


def per_device(
    velocity,
    density,
    tile_home,
    footprints,
    source_cell,
    source_wave,
    receivers,
    observed,
    pressure_old,
    pressure_now,
    adjoint_next,
    adjoint_now,
):
    owner_count = lax.axis_size("own")
    shot_count = lax.axis_size("shot")
    owner_index = lax.axis_index("own")
    shot_index = lax.axis_index("shot")
    tiles_held = velocity.shape[0]
    per_shot = footprints.shape[2]
    foot_tiles = footprints.shape[3]
    capacity = foot_tiles // owner_count
    positions = jnp.arange(foot_tiles)
    earlier = positions[None, :] < positions[:, None]
    wanted = owner_index * capacity + jnp.arange(capacity)
    plans = []
    for member in range(per_shot):
        home_rows = jnp.take(tile_home, footprints[:, :, member, :], axis=0)
        owners = home_rows // tiles_held
        ranks = jnp.sum((owners[..., :, None] == owners[..., None, :]) & earlier, axis=-1)
        slots = owners * capacity + ranks
        chosen = slots[..., None, :] == wanted[:, None]
        row_all = jnp.sum(
            jnp.where(chosen, home_rows[..., None, :] - owner_index * tiles_held, 0), axis=-1
        )
        row_mine = lax.dynamic_index_in_dim(row_all, shot_index, 1, keepdims=False)
        slot_rows = lax.dynamic_index_in_dim(slots, owner_index, 0, keepdims=False)
        own_slots = lax.dynamic_index_in_dim(slot_rows, shot_index, 0, keepdims=False)
        plans.append((row_all, row_mine, own_slots))
    velocity_out = [jnp.take(velocity, plan[1].reshape(-1), axis=0) for plan in plans]
    density_out = [jnp.take(density, plan[1].reshape(-1), axis=0) for plan in plans]
    arrivals = [
        (
            lax.all_to_all(velocity_out[member], "own", split_axis=0, concat_axis=0, tiled=True),
            lax.all_to_all(density_out[member], "own", split_axis=0, concat_axis=0, tiled=True),
        )
        for member in range(per_shot)
    ]
    tile_x, tile_y, depth = (velocity.shape[1], velocity.shape[2], velocity.shape[3])
    half_width = tile_x // shot_count
    gradient_sum = jnp.zeros((tiles_held, half_width, tile_y, depth), jnp.float32)
    for member in range(per_shot):
        row_all, row_mine, own_slots = plans[member]
        tile_velocity = jnp.take(arrivals[member][0], own_slots, axis=0)
        tile_density = jnp.take(arrivals[member][1], own_slots, axis=0)
        shot_velocity = tiles_to_field(tile_velocity, FT).astype(jnp.float32)
        shot_density = tiles_to_field(tile_density, FT).astype(jnp.float32)
        shot_gradient = run_shot(
            shot_velocity,
            shot_density,
            pressure_old[0, 0, member].astype(jnp.float32),
            pressure_now[0, 0, member].astype(jnp.float32),
            adjoint_next[0, 0, member].astype(jnp.float32),
            adjoint_now[0, 0, member].astype(jnp.float32),
            source_cell[0, 0, member],
            source_wave[0, 0, member],
            receivers[0, 0, member],
            observed[0, 0, member],
        )
        gradient_tiles = field_to_tiles(shot_gradient, FT)
        inverse = jnp.sum(
            jnp.where(own_slots[None, :] == positions[:, None], positions[None, :], 0), axis=1
        )
        ordered = jnp.take(gradient_tiles, inverse, axis=0)
        sectioned = ordered.reshape(
            owner_count, capacity, shot_count, half_width, tile_y, depth
        ).transpose(0, 2, 1, 3, 4, 5)
        sectioned = sectioned.reshape(
            owner_count * shot_count * capacity, half_width, tile_y, depth
        )
        arrived = lax.all_to_all(
            sectioned, ("own", "shot"), split_axis=0, concat_axis=0, tiled=True
        )
        gradient_sum = gradient_sum + place_rows(row_all.reshape(-1), arrived, tiles_held)
    return gradient_sum


def solution(mesh):
    in_specs = (
        P(("grp", "own"), None, None, None),
        P(("grp", "own"), None, None, None),
        P("grp"),
        P("grp", None, None, None),
        P(("grp", "own"), "shot", None),
        P(("grp", "own"), "shot", None, None),
        P(("grp", "own"), "shot", None, None),
        P(("grp", "own"), "shot", None, None, None),
        P(("grp", "own"), "shot", None, None, None, None),
        P(("grp", "own"), "shot", None, None, None, None),
        P(("grp", "own"), "shot", None, None, None, None),
        P(("grp", "own"), "shot", None, None, None, None),
    )
    out_specs = P(("grp", "own"), "shot", None, None)
    return jax.shard_map(
        per_device, mesh=mesh, in_specs=in_specs, out_specs=out_specs, check_vma=False
    )
```

profile of v0, /device:TPU:0, one launch (start us, length us, event | category | flops | bytes accessed | tf_op | source)
XLA Modules:
  0.0 185.0 jit_solution(16107887744428725134)
XLA Ops:
  0.0 0.8 fusion.609
  1.6 4.5 %gather_fusion.10 = s32[1024]{0:T(1024)S(1)} fusion(s32[1024]{0:T(1024)S(1)} %copy-done.1, s32[1024]{0:T(1024)S(1)} %broadcast_clamp_fusion), kind=kCustom, calls=%fused_computation.4.clone | custom fusion | bytes 12288 | tf_op jit(solution)/shard_map/jit(_take)/gather | solution.py:159
  6.3 4.5 %gather_fusion.4 = s32[1024]{0:T(1024)S(1)} fusion(s32[1024]{0:T(1024)S(1)} %copy-done.1, s32[1024]{0:T(1024)S(1)} %broadcast_clamp_fusion.1), kind=kCustom, calls=%fused_computation.clone | custom fusion | bytes 12288 | tf_op jit(solution)/shard_map/jit(_take)/gather | solution.py:159
  11.0 1.0 convert_reduce_fusion
  12.9 0.8 gather_fusion.7
  13.7 0.8 gather_fusion.5
  14.5 1.1 broadcast_select_fusion.8
  15.6 7.3 %all-to-all-start = ((bf16[64,4,4,128]{3,2,1,0:T(4,128)(2,1)}), bf16[64,4,4,128]{3,2,1,0:T(4,128)(2,1)S(1)}, u32[]{:S(2)}, u32[]{:S(2)}) async-start(bf16[64,4,4,128]{3,2,1,0:T(4,128)(2,1)} %get-tuple-element.150), calls=%async_computation | async-start | bytes 524288 | tf_op jit(solution)/shard_map/all_to_all | solution.py:175
  23.0 0.8 gather_fusion.13
  23.8 0.8 gather_fusion.11
  26.2 1.1 broadcast_select_fusion.4
  27.3 4.5 %all-to-all-done = bf16[64,4,4,128]{3,2,1,0:T(4,128)(2,1)S(1)} async-done(((bf16[64,4,4,128]{3,2,1,0:T(4,128)(2,1)}), bf16[64,4,4,128]{3,2,1,0:T(4,128)(2,1)S(1)}, u32[]{:S(2)}, u32[]{:S(2)}) %all-to-all-start) | async-done | bytes 262176 | tf_op jit(solution)/shard_map/all_to_all | solution.py:175
  32.6 3.7 %all-to-all-start.3 = ((bf16[64,4,4,128]{3,2,1,0:T(4,128)(2,1)}), bf16[64,4,4,128]{3,2,1,0:T(4,128)(2,1)S(1)}, u32[]{:S(2)}, u32[]{:S(2)}) async-start(bf16[64,4,4,128]{3,2,1,0:T(4,128)(2,1)} %get-tuple-element.148), calls=%async_computation.3 | async-start | bytes 524288 | tf_op jit(solution)/shard_map/all_to_all | solution.py:175
  41.4 3.4 %all-to-all-done.3 = bf16[64,4,4,128]{3,2,1,0:T(4,128)(2,1)S(1)} async-done(((bf16[64,4,4,128]{3,2,1,0:T(4,128)(2,1)}), bf16[64,4,4,128]{3,2,1,0:T(4,128)(2,1)S(1)}, u32[]{:S(2)}, u32[]{:S(2)}) %all-to-all-start.3) | async-done | bytes 262176 | tf_op jit(solution)/shard_map/all_to_all | solution.py:175
  44.8 3.6 %all-to-all-start.4 = ((bf16[64,4,4,128]{3,2,1,0:T(4,128)(2,1)}), bf16[64,4,4,128]{3,2,1,0:T(4,128)(2,1)S(1)}, u32[]{:S(2)}, u32[]{:S(2)}) async-start(bf16[64,4,4,128]{3,2,1,0:T(4,128)(2,1)} %get-tuple-element.147), calls=%async_computation.4 | async-start | bytes 524288 | tf_op jit(solution)/shard_map/all_to_all | solution.py:176
  48.5 0.9 bitcast_convert_fusion
  49.5 1.1 bitcast_convert_fusion.1
  50.6 6.3 %all-to-all-done.4 = bf16[64,4,4,128]{3,2,1,0:T(4,128)(2,1)S(1)} async-done(((bf16[64,4,4,128]{3,2,1,0:T(4,128)(2,1)}), bf16[64,4,4,128]{3,2,1,0:T(4,128)(2,1)S(1)}, u32[]{:S(2)}, u32[]{:S(2)}) %all-to-all-start.4) | async-done | bytes 262176 | tf_op jit(solution)/shard_map/all_to_all | solution.py:176
  57.0 4.2 %all-to-all-start.1 = ((bf16[64,4,4,128]{3,2,1,0:T(4,128)(2,1)}), bf16[64,4,4,128]{3,2,1,0:T(4,128)(2,1)}, u32[]{:S(2)}, u32[]{:S(2)}) async-start(bf16[64,4,4,128]{3,2,1,0:T(4,128)(2,1)} %get-tuple-element.149), calls=%async_computation.1 | async-start | bytes 524288 | tf_op jit(solution)/shard_map/all_to_all | solution.py:176
  61.2 0.8 gather_fusion.12
  62.0 0.8 gather_fusion.14
  62.8 1.2 convert_multiply_fusion
  64.2 1.0 slice.1627
  65.2 1.0 slice.1626
  66.2 0.8 slice.1622
  67.0 0.9 slice.1624
  68.0 0.8 gather_fusion.6
  69.3 2.4 %gather_fusion.8 = bf16[64,4,4,128]{3,2,1,0:T(4,128)(2,1)} fusion(bf16[64,4,4,128]{3,2,1,0:T(4,128)(2,1)} %all-to-all-done.1, s32[1024]{0:T(1024)S(1)} %pad_clamp_fusion.6), kind=kCustom, calls=%fused_computation.8.clone | custom fusion | bytes 524544 | tf_op jit(solution)/shard_map/jit(_take)/gather | solution.py:186
  71.7 1.4 convert_multiply_fusion.2
  73.8 0.9 copy.78
  76.3 2.3 %fusion.70 = (f32[32,32,128]{2,1,0:T(8,128)S(1)}, f32[32,32,128]{2,1,0:T(8,128)}, f32[32,32,128]{2,1,0:T(8,128)S(1)}, f32[32,32,128]{2,1,0:T(8,128)}, f32[32,32,128]{2,1,0:T(8,128)S(1)}, /*index=5*/f32[32,32,128]{2,1,0:T(8,128)}) fusion(f32[32,32,128]{2,1,0:T(8,128)S(1)} %copy-done.14, bf16[1,1,2,32,32,128]{5,4,3,2,1,0:T(8,128)(2,1)S(1)} %copy-done.2, ...), kind=kLoop, calls=%fused_computation.457 | loop fusion | flops 6029312 | bytes 6029312 | tf_op jit(solution)/shard_map/mul | solution.py:46
  78.6 2.4 %fusion.34 = (f32[32,32,128]{2,1,0:T(8,128)S(1)}, f32[32,32,128]{2,1,0:T(8,128)}, f32[32,32,128]{2,1,0:T(8,128)S(1)}, f32[32,32,128]{2,1,0:T(8,128)}, f32[32,32,128]{2,1,0:T(8,128)S(1)}, /*index=5*/f32[32,32,128]{2,1,0:T(8,128)}) fusion(f32[32,32,128]{2,1,0:T(8,128)S(1)} %get-tuple-element.123, bf16[1,1,2,32,32,128]{5,4,3,2,1,0:T(8,128)(2,1)S(1)} %copy-done.2, ...), kind=kLoop, calls=%fused_computation.421 | loop fusion | flops 6029312 | bytes 6029312 | tf_op jit(solution)/shard_map/mul | solution.py:46
  81.0 3.6 %fusion.55 = (f32[32,32,128]{2,1,0:T(8,128)S(1)}, f32[32,32,128]{2,1,0:T(8,128)}, f32[32,32,128]{2,1,0:T(8,128)S(1)}, f32[32,32,128]{2,1,0:T(8,128)}) fusion(f32[32,32,128]{2,1,0:T(8,128)S(1)} %bitcast.188, bf16[1,1,2,32,32,128]{5,4,3,2,1,0:T(8,128)(2,1)S(1)} %copy-done.26, bf16[1,1,2,32,32,128]{5,4,3,2,1,0:T(8,128)(2,1)S(1)} %copy-done.2, ...), kind=kLoop, calls=%fused_computation.442 | loop fusion | flops 10747904 | bytes 7340032 | tf_op jit(solution)/shard_map/add | solution.py:81
  84.6 0.8 fusion.591
  85.4 1.1 gather_fusion.3
  86.5 0.8 fusion.589
  87.4 1.1 gather_fusion.1
  88.6 10.1 %fusion.52 = (f32[32,32,128]{2,1,0:T(8,128)}, f32[32,32,128]{2,1,0:T(8,128)}, f32[32,32,128]{2,1,0:T(8,128)}, f32[32,32,128]{2,1,0:T(8,128)S(1)}, f32[32,32,128]{2,1,0:T(8,128)S(1)}, /*index=5*/f32[32,32,128]{2,1,0:T(8,128)S(1)}) fusion(f32[32,32,128]{2,1,0:T(8,128)} %get-tuple-element.66, f32[32,32,128]{2,1,0:T(8,128)} %get-tuple-element.120, ...), kind=kLoop, calls=%fused_computation.439 | loop fusion | flops 9568256 | bytes 6029312 | tf_op jit(solution)/shard_map/mul | solution.py:46
  98.7 3.6 %fusion.16 = (f32[32,32,128]{2,1,0:T(8,128)}, f32[32,32,128]{2,1,0:T(8,128)}, f32[32,32,128]{2,1,0:T(8,128)}, f32[32,32,128]{2,1,0:T(8,128)S(1)}, f32[32,32,128]{2,1,0:T(8,128)S(1)}, /*index=5*/f32[32,32,128]{2,1,0:T(8,128)S(1)}) fusion(f32[32,32,128]{2,1,0:T(8,128)S(1)} %copy-done.6, f32[32,32,128]{2,1,0:T(8,128)S(1)} %copy-done.13, ...), kind=kLoop, calls=%fused_computation.403 | loop fusion | flops 9568256 | bytes 6029312 | tf_op jit(solution)/shard_map/mul | solution.py:46
  102.3 3.8 %fusion.71 = (f32[32,32,128]{2,1,0:T(8,128)}, f32[32,32,128]{2,1,0:T(8,128)}, f32[32,32,128]{2,1,0:T(8,128)}, f32[32,32,128]{2,1,0:T(8,128)}) fusion(f32[32,32,128]{2,1,0:T(8,128)S(1)} %bitcast.189, f32[32,32,128]{2,1,0:T(8,128)S(1)} %bitcast.201, bf16[1,1,2,32,32,128]{5,4,3,2,1,0:T(8,128)(2,1)S(1)} %copy-done.2, f32[32,32,128]{2,1,0:T(8,128)S(1)} %get-tuple-element.112, ...), kind=kLoop, calls=%fused_computation.458 | loop fusion | flops 10485760 | bytes 7864320 | tf_op jit(solution)/shard_map/add | solution.py:85
  106.0 2.2 %fusion.590 = f32[131072]{0:T(1024)} fusion(f32[131072]{0:T(1024)} %bitcast.29, s32[]{:T(128)S(6)} %select_n.105, pred[1]{0:T(512)(128)(4,1)} %bitcast.26, f32[1,1,1,1]{3,2,1,0:T(1,128)} %get-tuple-element.140), kind=kLoop, calls=%fused_computation.1058 | loop fusion | flops 2 | bytes 2052 | tf_op jit(solution)/shard_map/scatter-add | solution.py:57
  108.2 2.0 %gather_fusion = f32[128]{0:T(128)S(1)} fusion(f32[131072]{0:T(1024)} %fusion.590, s32[1024]{0:T(1024)S(1)} %get-tuple-element.158), kind=kCustom, calls=%fused_computation.12 | custom fusion | bytes 1536 | tf_op jit(solution)/shard_map/gather | solution.py:61
  110.2 0.8 fusion.592
  111.0 1.1 gather_fusion.2
  112.2 12.4 %fusion.37 = (f32[32,32,128]{2,1,0:T(8,128)S(1)}, f32[32,32,128]{2,1,0:T(8,128)S(1)}) fusion(f32[32,32,128]{2,1,0:T(8,128)S(1)} %bitcast.190, f32[32,32,128]{2,1,0:T(8,128)} %get-tuple-element.98, f32[32,32,128]{2,1,0:T(8,128)} %get-tuple-element.99, f32[32,32,128]{2,1,0:T(8,128)} %get-tuple-element.97, bf16[1,1,2,32,32,128]{5,4,3,2,1,0:T(8,128)(2,1)} %param.38, ...), kind=kLoop, calls=%fused_computation.424 | loop fusion | flops 10747904 | bytes 6291456 | tf_op jit(solution)/shard_map/add | solution.py:90
  124.6 1.5 scatter_fusion.2
  126.1 3.5 %fusion.559 = (f32[32,32,128]{2,1,0:T(8,128)}, f32[32,32,128]{2,1,0:T(8,128)}, f32[32,32,128]{2,1,0:T(8,128)}) fusion(f32[32,32,128]{2,1,0:T(8,128)} %get-tuple-element.66, f32[32,32,128]{2,1,0:T(8,128)S(1)} %bitcast.185, f32[32,32,128]{2,1,0:T(8,128)} %get-tuple-element.88, f32[32,32,128]{2,1,0:T(8,128)} %get-tuple-element.86), kind=kLoop, calls=%fused_computation.946 | loop fusion | flops 4718592 | bytes 3670016 | tf_op jit(solution)/shard_map/mul | solution.py:46
  129.6 1.7 scatter_fusion
  131.4 2.5 %fusion.491 = (f32[32,32,128]{2,1,0:T(8,128)S(1)}, f32[32,32,128]{2,1,0:T(8,128)S(1)}, f32[32,32,128]{2,1,0:T(8,128)S(1)}) fusion(f32[32,32,128]{2,1,0:T(8,128)} %get-tuple-element.78, f32[32,32,128]{2,1,0:T(8,128)S(1)} %bitcast.181, f32[32,32,128]{2,1,0:T(8,128)} %get-tuple-element.92, f32[32,32,128]{2,1,0:T(8,128)} %get-tuple-element.90), kind=kLoop, calls=%fused_computation.878 | loop fusion | flops 4718592 | bytes 3670016 | tf_op jit(solution)/shard_map/mul | solution.py:46
  133.9 3.6 %fusion.53 = (f32[32,32,128]{2,1,0:T(8,128)}, f32[32,32,128]{2,1,0:T(8,128)}) fusion(f32[32,32,128]{2,1,0:T(8,128)S(1)} %bitcast.191, f32[32,32,128]{2,1,0:T(8,128)S(1)} %copy-done.22, f32[32,32,128]{2,1,0:T(8,128)S(1)} %copy-done.21, f32[32,32,128]{2,1,0:T(8,128)S(1)} %copy-done.20, f32[32,32,128]{2,1,0:T(8,128)S(1)} %bitcast.186, ...), kind=kLoop, calls=%fused_computation.440 | loop fusion | flops 10485760 | bytes 6815744 | tf_op jit(solution)/shard_map/add | solution.py:95
  137.5 3.1 %scatter_fusion.1 = f32[131072]{0:T(1024)} fusion(f32[131072]{0:T(1024)} %bitcast.204, s32[128]{0:T(128)S(1)} %get-tuple-element.144, f32[128]{0:T(128)S(1)} %get-tuple-element.136), kind=kCustom, calls=%fused_computation.17 | custom fusion | flops 128 | bytes 2048 | tf_op jit(solution)/shard_map/scatter-add | solution.py:57
  140.7 1.5 add_multiply_fusion.1
  142.6 0.9 gather_fusion.9
  143.8 1.1 copy.85
  145.0 5.5 %all-to-all-start.2 = ((f32[128,2,4,128]{3,2,1,0:T(4,128)}), f32[128,2,4,128]{3,2,1,0:T(4,128)S(1)}, u32[]{:S(2)}, u32[]{:S(2)}) async-start(f32[128,2,4,128]{3,2,1,0:T(4,128)} %copy.85), calls=%async_computation.2 | async-start | bytes 1048576 | tf_op jit(solution)/shard_map/all_to_all | solution.py:212
  150.6 0.9 copy-done.9
  151.5 1.5 scatter_fusion.3
  153.0 1.3 add_multiply_fusion
  154.8 0.9 gather_fusion.15
  156.0 1.1 copy.95
  157.2 7.6 %all-to-all-done.2 = f32[128,2,4,128]{3,2,1,0:T(4,128)S(1)} async-done(((f32[128,2,4,128]{3,2,1,0:T(4,128)}), f32[128,2,4,128]{3,2,1,0:T(4,128)S(1)}, u32[]{:S(2)}, u32[]{:S(2)}) %all-to-all-start.2) | async-done | bytes 524320 | tf_op jit(solution)/shard_map/all_to_all | solution.py:212
  164.7 4.2 %all-to-all-start.5 = ((f32[128,2,4,128]{3,2,1,0:T(4,128)}), f32[128,2,4,128]{3,2,1,0:T(4,128)S(1)}, u32[]{:S(2)}, u32[]{:S(2)}) async-start(f32[128,2,4,128]{3,2,1,0:T(4,128)} %copy.95), calls=%async_computation.5 | async-start | bytes 1048576 | tf_op jit(solution)/shard_map/all_to_all | solution.py:212
  169.8 13.4 %all-to-all-done.5 = f32[128,2,4,128]{3,2,1,0:T(4,128)S(1)} async-done(((f32[128,2,4,128]{3,2,1,0:T(4,128)}), f32[128,2,4,128]{3,2,1,0:T(4,128)S(1)}, u32[]{:S(2)}, u32[]{:S(2)}) %all-to-all-start.5) | async-done | bytes 524320 | tf_op jit(solution)/shard_map/all_to_all | solution.py:212
  183.9 1.1 copy.97
  (134 shorter events, 11.8 us)
Async XLA Ops:
  0.0 12.9 %copy-start = (bf16[128,4,4,128]{3,2,1,0:T(4,128)(2,1)S(1)}, bf16[128,4,4,128]{3,2,1,0:T(4,128)(2,1)}, u32[]{:S(2)}) copy-start(bf16[128,4,4,128]{3,2,1,0:T(4,128)(2,1)} %param.29) | copy-start | bytes 1572868
  0.9 0.7 copy-start.1
  10.8 2.9 %copy-start.27 = (bf16[128,4,4,128]{3,2,1,0:T(4,128)(2,1)S(1)}, bf16[128,4,4,128]{3,2,1,0:T(4,128)(2,1)}, u32[]{:S(2)}) copy-start(bf16[128,4,4,128]{3,2,1,0:T(4,128)(2,1)} %param.28) | copy-start | bytes 1572868
  15.6 16.2 %all-to-all-start = ((bf16[64,4,4,128]{3,2,1,0:T(4,128)(2,1)}), bf16[64,4,4,128]{3,2,1,0:T(4,128)(2,1)S(1)}, u32[]{:S(2)}, u32[]{:S(2)}) async-start(bf16[64,4,4,128]{3,2,1,0:T(4,128)(2,1)} %get-tuple-element.150), calls=%async_computation | async-start | bytes 524288 | tf_op jit(solution)/shard_map/all_to_all | solution.py:175
  24.9 0.7 copy-start.30
  31.9 0.7 copy-start.24
  32.6 8.2 %copy-start.28 = (f32[1,1,2,2]{3,2,1,0:T(2,128)S(1)}, f32[1,1,2,2]{3,2,1,0:T(2,128)}, u32[]{:S(2)}) copy-start(f32[1,1,2,2]{3,2,1,0:T(2,128)} %param.33) | copy-start | bytes 52
  32.6 15.9 %copy-start.2 = (bf16[1,1,2,32,32,128]{5,4,3,2,1,0:T(8,128)(2,1)S(1)}, bf16[1,1,2,32,32,128]{5,4,3,2,1,0:T(8,128)(2,1)}, u32[]{:S(2)}) copy-start(bf16[1,1,2,32,32,128]{5,4,3,2,1,0:T(8,128)(2,1)} %param.37) | copy-start | bytes 1572868
  32.6 12.3 %all-to-all-start.3 = ((bf16[64,4,4,128]{3,2,1,0:T(4,128)(2,1)}), bf16[64,4,4,128]{3,2,1,0:T(4,128)(2,1)S(1)}, u32[]{:S(2)}, u32[]{:S(2)}) async-start(bf16[64,4,4,128]{3,2,1,0:T(4,128)(2,1)} %get-tuple-element.148), calls=%async_computation.3 | async-start | bytes 524288 | tf_op jit(solution)/shard_map/all_to_all | solution.py:175
  40.1 0.7 copy-start.31
  44.8 12.1 %all-to-all-start.4 = ((bf16[64,4,4,128]{3,2,1,0:T(4,128)(2,1)}), bf16[64,4,4,128]{3,2,1,0:T(4,128)(2,1)S(1)}, u32[]{:S(2)}, u32[]{:S(2)}) async-start(bf16[64,4,4,128]{3,2,1,0:T(4,128)(2,1)} %get-tuple-element.147), calls=%async_computation.4 | async-start | bytes 524288 | tf_op jit(solution)/shard_map/all_to_all | solution.py:176
  48.4 1.0 copy-start.3
  57.0 12.3 %all-to-all-start.1 = ((bf16[64,4,4,128]{3,2,1,0:T(4,128)(2,1)}), bf16[64,4,4,128]{3,2,1,0:T(4,128)(2,1)}, u32[]{:S(2)}, u32[]{:S(2)}) async-start(bf16[64,4,4,128]{3,2,1,0:T(4,128)(2,1)} %get-tuple-element.149), calls=%async_computation.1 | async-start | bytes 524288 | tf_op jit(solution)/shard_map/all_to_all | solution.py:176
  67.0 1.0 copy-start.25
  73.8 1.2 copy-start.23
  74.7 1.1 copy-start.17
  74.7 1.2 copy-start.18
  74.8 1.2 copy-start.14
  74.9 1.4 copy-start.16
  78.6 2.4 %copy-start.26 = (bf16[1,1,2,32,32,128]{5,4,3,2,1,0:T(8,128)(2,1)S(1)}, bf16[1,1,2,32,32,128]{5,4,3,2,1,0:T(8,128)(2,1)}, u32[]{:S(2)}) copy-start(bf16[1,1,2,32,32,128]{5,4,3,2,1,0:T(8,128)(2,1)} %param.36) | copy-start | bytes 1572868
  88.5 10.1 %copy-start.4 = (bf16[1,1,2,32,32,128]{5,4,3,2,1,0:T(8,128)(2,1)S(1)}, bf16[1,1,2,32,32,128]{5,4,3,2,1,0:T(8,128)(2,1)}, u32[]{:S(2)}) copy-start(bf16[1,1,2,32,32,128]{5,4,3,2,1,0:T(8,128)(2,1)} %param.39) | copy-start | bytes 1572868
  88.5 10.1 %copy-start.6 = (f32[32,32,128]{2,1,0:T(8,128)S(1)}, f32[32,32,128]{2,1,0:T(8,128)}, u32[]{:S(2)}) copy-start(f32[32,32,128]{2,1,0:T(8,128)} %get-tuple-element.78) | copy-start | bytes 1572868
  88.6 10.1 %copy-start.7 = (f32[32,32,128]{2,1,0:T(8,128)S(1)}, f32[32,32,128]{2,1,0:T(8,128)}, u32[]{:S(2)}) copy-start(f32[32,32,128]{2,1,0:T(8,128)} %get-tuple-element.90) | copy-start | bytes 1572868
  88.6 10.1 %copy-start.8 = (f32[32,32,128]{2,1,0:T(8,128)S(1)}, f32[32,32,128]{2,1,0:T(8,128)}, u32[]{:S(2)}) copy-start(f32[32,32,128]{2,1,0:T(8,128)} %get-tuple-element.92) | copy-start | bytes 1572868
  88.6 10.1 %copy-start.13 = (f32[32,32,128]{2,1,0:T(8,128)S(1)}, f32[32,32,128]{2,1,0:T(8,128)}, u32[]{:S(2)}) copy-start(f32[32,32,128]{2,1,0:T(8,128)} %get-tuple-element.121) | copy-start | bytes 1572868
  106.0 4.2 %copy-start.10 = (f32[32,32,128]{2,1,0:T(8,128)S(1)}, f32[32,32,128]{2,1,0:T(8,128)}, u32[]{:S(2)}) copy-start(f32[32,32,128]{2,1,0:T(8,128)} %get-tuple-element.61) | copy-start | bytes 1572868
  108.2 4.0 %copy-start.5 = (bf16[1,1,2,32,32,128]{5,4,3,2,1,0:T(8,128)(2,1)S(1)}, bf16[1,1,2,32,32,128]{5,4,3,2,1,0:T(8,128)(2,1)}, u32[]{:S(2)}) copy-start(bf16[1,1,2,32,32,128]{5,4,3,2,1,0:T(8,128)(2,1)} %param.39) | copy-start | bytes 1572868
  111.0 1.2 copy-start.29
  131.3 2.6 %copy-start.20 = (f32[32,32,128]{2,1,0:T(8,128)S(1)}, f32[32,32,128]{2,1,0:T(8,128)}, u32[]{:S(2)}) copy-start(f32[32,32,128]{2,1,0:T(8,128)} %get-tuple-element.115) | copy-start | bytes 1572868
  131.4 2.6 %copy-start.21 = (f32[32,32,128]{2,1,0:T(8,128)S(1)}, f32[32,32,128]{2,1,0:T(8,128)}, u32[]{:S(2)}) copy-start(f32[32,32,128]{2,1,0:T(8,128)} %get-tuple-element.116) | copy-start | bytes 1572868
  131.4 2.6 %copy-start.22 = (f32[32,32,128]{2,1,0:T(8,128)S(1)}, f32[32,32,128]{2,1,0:T(8,128)}, u32[]{:S(2)}) copy-start(f32[32,32,128]{2,1,0:T(8,128)} %get-tuple-element.117) | copy-start | bytes 1572868
  137.5 3.2 %copy-start.12 = (f32[32,32,128]{2,1,0:T(8,128)S(1)}, f32[32,32,128]{2,1,0:T(8,128)}, u32[]{:S(2)}) copy-start(f32[32,32,128]{2,1,0:T(8,128)} %get-tuple-element.94) | copy-start | bytes 1572868
  137.5 3.2 %copy-start.19 = (f32[8,8,4,4,128]{4,3,1,2,0:T(4,128)S(1)}, f32[8,8,4,4,128]{4,3,1,2,0:T(4,128)}, u32[]{:S(2)}) copy-start(f32[8,8,4,4,128]{4,3,1,2,0:T(4,128)} %copy.78) | copy-start | bytes 1572868
  145.0 5.5 %copy-start.15 = (f32[64,4,4,128]{3,2,1,0:T(4,128)S(1)}, f32[64,4,4,128]{3,2,1,0:T(4,128)}, u32[]{:S(2)}) copy-start(f32[64,4,4,128]{3,2,1,0:T(4,128)} %get-tuple-element.104) | copy-start | bytes 1572868
  145.0 19.8 %all-to-all-start.2 = ((f32[128,2,4,128]{3,2,1,0:T(4,128)}), f32[128,2,4,128]{3,2,1,0:T(4,128)S(1)}, u32[]{:S(2)}, u32[]{:S(2)}) async-start(f32[128,2,4,128]{3,2,1,0:T(4,128)} %copy.85), calls=%async_computation.2 | async-start | bytes 1048576 | tf_op jit(solution)/shard_map/all_to_all | solution.py:212
  150.5 1.0 copy-start.9
  151.5 1.5 copy-start.11
  164.7 18.4 %all-to-all-start.5 = ((f32[128,2,4,128]{3,2,1,0:T(4,128)}), f32[128,2,4,128]{3,2,1,0:T(4,128)S(1)}, u32[]{:S(2)}, u32[]{:S(2)}) async-start(f32[128,2,4,128]{3,2,1,0:T(4,128)} %copy.95), calls=%async_computation.5 | async-start | bytes 1048576 | tf_op jit(solution)/shard_map/all_to_all | solution.py:212
where the time goes:
time: 186 us; the launch traced here: 185 us
  other arithmetic  72.4 us (39%)
  local copies, waits for them, and re-layouts  42.8 us (23%)
  waiting for transfers between devices  35.8 us (19%)
  starting transfers between devices  28.5 us (15%)
  between operations  4.65 us (3%)
    mul x6, other arithmetic, apply_operator(): flux_pad = pad_along(half_buoys[dimension] * gradient, dimension)  24.3 us
    all_to_all x2, waiting for transfers between devices, per_device(): lax.all_to_all(sectioned, ('own', 'shot'), split_axis=0, concat_axis=0, t...  21 us
    scatter-add x8, other arithmetic, inject(): wavefield.reshape(-1).at[cell_index].add(amounts).reshape(wavefield.shape)  12.5 us
    add x1, other arithmetic, run_shot(): 2.0 * adjoint_now - adjoint_next  12.4 us
    all_to_all x2, starting transfers between devices, per_device(): lax.all_to_all(velocity_out[member], 'own', split_axis=0, concat_axis=0,...  11 us
    all_to_all x2, starting transfers between devices, per_device(): lax.all_to_all(sectioned, ('own', 'shot'), split_axis=0, concat_axis=0, t...  9.66 us
    gather x4, local copies, waits for them, and re-layouts, per_device(): home_rows = jnp.take(tile_home, footprints[:, :, member, :], axis=0)  9.2 us
    all_to_all x2, waiting for transfers between devices, per_device(): lax.all_to_all(velocity_out[member], 'own', split_axis=0, concat_axis=0,...  7.95 us
  transfers between devices with their start and end apart: 6, of which 6 were waited for; matrix products, arithmetic and copies ran while one was open for 11% of the time, Pallas kernels for 0%

commit v1 on v0

v1 whole, which is shorter than its diff:
```python
import functools

import jax
import jax.numpy as jnp
import numpy as np
from jax import lax
from jax.experimental import pallas as pl
from jax.experimental.pallas import tpu as pltpu
from jax.sharding import PartitionSpec as P

COURANT = 0.09
LEAD = 1225.0 / 1024.0
RATIOS = (1.0, -1.0 / 15.0, 1.0 / 125.0, -1.0 / 1715.0)
BAND = 105.0
YOFF = 8


def band_matrices(depth):
    grad = np.zeros((depth, depth), np.float32)
    for i in range(depth):
        for m, ratio in enumerate(RATIOS, start=1):
            if i + m < depth:
                grad[i + m, i] += BAND * ratio
            if i + 1 - m >= 0:
                grad[i + 1 - m, i] -= BAND * ratio
    div = np.zeros((depth, depth), np.float32)
    for i in range(depth):
        for m, ratio in enumerate(RATIOS, start=1):
            if i + m - 1 < depth:
                div[i + m - 1, i] += BAND * ratio
            if i - m >= 0:
                div[i - m, i] -= BAND * ratio
    stack = lambda a: np.concatenate([a, a], axis=0)
    return jnp.asarray(np.stack([stack(grad), stack(div)]), jnp.bfloat16)


def gather_kernel(rows_ref, v_ref, d_ref, *outs):
    owners, _, cap = outs[0].shape[:3]
    for member, out in enumerate(outs):
        def body(dest, carry):
            for j in range(cap):
                row = rows_ref[(member * owners + dest) * cap + j]
                out[dest, 0, j] = v_ref[row]
                out[dest, 1, j] = d_ref[row]
            return carry

        lax.fori_loop(0, owners, body, 0)


def scatter_kernel(rows_ref, *refs):
    arrived, out = refs[:-1], refs[-1]
    out[...] = jnp.zeros_like(out)
    for member, ref in enumerate(arrived):
        sources, cap = ref.shape[:2]

        def body(src, carry):
            for j in range(cap):
                row = rows_ref[(member * sources + src) * cap + j]
                out[row] = out[row] + ref[src, j]
            return carry

        lax.fori_loop(0, sources, body, 0)


def taps(at, low):
    total = None
    for m, ratio in enumerate(RATIOS, start=1):
        up, down = (at(m), at(1 - m)) if low else (at(m - 1), at(-m))
        if up is None and down is None:
            continue
        diff = up - down if up is not None and down is not None else (up if down is None else -down)
        term = diff if m == 1 else ratio * diff
        total = term if total is None else total + term
    return total


def split(value):
    high = value.astype(jnp.bfloat16)
    low = (value - high.astype(jnp.float32)).astype(jnp.bfloat16)
    return jnp.concatenate([high, low], axis=-1)


def shot_kernel(
    slots_ref, source_ref, recv_cells, wave_ref, obs_ref,
    tiles_ref, band_ref, old_ref, now_ref, next_ref, adj_ref,
    out_ref,
    vel, rho, buoy, hx, hy, hz, fy, div_z, pad_u, pad_w, image_one, image_two, third, inject_zero,
):
    nx, ny, nz = now_ref.shape[-3:]
    cap = tiles_ref.shape[2]
    grid_y = ny // 4
    tiles_y = ny // 8
    lane = lax.broadcasted_iota(jnp.int32, (1, nz), 1)
    rows = nx * 8

    def place(kx, carry):
        for ky in range(grid_y):
            slot = slots_ref[kx * grid_y + ky]
            for which, field in ((0, vel), (1, rho)):
                tile = tiles_ref[slot // cap, which, slot % cap].astype(jnp.float32)
                for i in range(4):
                    field[kx * 4 + i, pl.ds(ky * 4, 4), :] = tile[4 * i : 4 * i + 4]
        return carry

    lax.fori_loop(0, nx // 4, place, 0)

    zero_edge = jnp.zeros((nx, YOFF, nz), jnp.float32)
    for ref in (pad_u, pad_w, fy):
        ref[:, pl.ds(0, YOFF), :] = zero_edge
        ref[:, pl.ds(YOFF + ny, YOFF), :] = zero_edge

    def prepare(x, carry):
        value = (0.5 * LEAD * LEAD) / rho[x]
        buoy[x, pl.ds(0, ny), :] = value
        buoy[x, pl.ds(ny, 1), :] = value[ny - 1 :]
        pad_u[x, pl.ds(YOFF, ny), :] = now_ref[0, 0, 0, x].astype(jnp.float32)
        pad_w[x, pl.ds(YOFF, ny), :] = adj_ref[0, 0, 0, x].astype(jnp.float32)
        return carry

    lax.fori_loop(0, nx, prepare, 0, unroll=2)

    def halves(x, carry):
        here = buoy[x, pl.ds(0, ny), :]
        after = buoy[jnp.minimum(x + 1, nx - 1), pl.ds(0, ny), :]
        hx[x] = here + after
        hy[x] = here + buoy[x, pl.ds(1, ny), :]
        shifted = jnp.where(lane == nz - 1, here, pltpu.roll(here, nz - 1, 1))
        hz[x] = (here + shifted) * (1.0 / (BAND * BAND))
        velocity, density = vel[x], rho[x]
        vel[x] = (COURANT * velocity) * (COURANT * velocity) * density
        rho[x] = (2.0 * COURANT * COURANT) * velocity * density
        return carry

    lax.fori_loop(0, nx, halves, 0, unroll=2)

    def operate(field, exact, finish):
        def flux_y(x, carry):
            at = lambda shift: field[x, pl.ds(YOFF + shift, ny), :]
            fy[x, pl.ds(YOFF, ny), :] = hy[x] * taps(at, True)
            return carry

        lax.fori_loop(0, nx, flux_y, 0, unroll=2)

        def tile_loop(ty, carry):
            start = pl.multiple_of(ty * 8, 8)
            here = pl.ds(start, 8)
            padded = pl.ds(pl.multiple_of(start + YOFF, 8), 8)
            block = field[:, padded, :].reshape(rows, nz)
            if exact:
                grad_z = jnp.dot(block.astype(jnp.bfloat16), band_ref[0, :nz], preferred_element_type=jnp.float32)
            else:
                grad_z = jnp.dot(split(block), band_ref[0], preferred_element_type=jnp.float32)
            flux_z = hz[:, here, :].reshape(rows, nz) * grad_z
            div_z[...] = jnp.dot(split(flux_z), band_ref[1], preferred_element_type=jnp.float32).reshape(nx, 8, nz)
            values, fluxes = {}, {}

            def value_at(x):
                if x < 0 or x >= nx:
                    return None
                if x not in values:
                    values[x] = field[x, padded, :]
                return values[x]

            def flux_at(x):
                if x < 0 or x >= nx:
                    return None
                if x not in fluxes:
                    fluxes[x] = hx[x, here, :] * taps(lambda shift: value_at(x + shift), True)
                return fluxes[x]

            for x in range(nx):
                total = taps(lambda shift: flux_at(x + shift), False)
                total = total + taps(lambda shift: fy[x, pl.ds(start + YOFF + shift, 8), :], False)
                total = total + div_z[x]
                finish(x, ty, here, padded, value_at(x), total)
            return carry

        lax.fori_loop(0, tiles_y, tile_loop, 0)

    def add_at(field, offset, cell, amount):
        row, z = cell // nz, cell % nz
        x, y = row // ny, row % ny + offset
        field[x, pl.ds(y, 1), :] += jnp.where(lane == z, amount, 0.0)

    second = pad_w

    def finish_one(x, ty, here, padded, value, total):
        image_one[x, here, :] = total
        third[x, padded, :] = 2.0 * value - old_ref[0, 0, 0, x, here, :].astype(jnp.float32) + vel[x, here, :] * total

    third[:, pl.ds(0, YOFF), :] = zero_edge
    third[:, pl.ds(YOFF + ny, YOFF), :] = zero_edge
    operate(pad_u, True, finish_one)
    add_at(third, YOFF, source_ref[0], wave_ref[0])

    def finish_two(x, ty, here, padded, value, total):
        image_two[x, here, :] = total
        pad_u[x, padded, :] = 2.0 * value - pad_u[x, padded, :] + vel[x, here, :] * total

    operate(third, False, finish_two)
    add_at(pad_u, YOFF, source_ref[0], wave_ref[1])

    q1 = buoy_q1 = inject_zero

    minus_q2 = hz_free = None

    def finish_three(x, ty, here, padded, value, total):
        q1[x, padded, :] = 2.0 * value - next_ref[0, 0, 0, x, here, :].astype(jnp.float32) + vel[x, here, :] * total

    q1[:, pl.ds(0, YOFF), :] = zero_edge
    q1[:, pl.ds(YOFF + ny, YOFF), :] = zero_edge
    operate(second, True, finish_three)

    count = recv_cells.shape[0]

    def receive(step, carry):
        for sub in range(8):
            n = step * 8 + sub
            cell = recv_cells[n]
            row, z = cell // nz, cell % nz
            x, y = row // ny, row % ny + YOFF
            spot = pl.ds(y, 1)
            pick = lane == z
            q1[x, spot, :] += jnp.where(pick, pad_u[x, spot, :] - obs_ref[count + n], 0.0)
            second[x, spot, :] -= jnp.where(pick, third[x, spot, :] - obs_ref[n], 0.0)
        return carry

    lax.fori_loop(0, count // 8, receive, 0)

    def finish_four(x, ty, here, padded, value, total):
        q0 = 2.0 * value - second[x, padded, :] + vel[x, here, :] * total
        result = rho[x, here, :] * (value * image_two[x, here, :] + q0 * image_one[x, here, :])
        for half in range(2):
            slot = slots_ref[(x // 4) * grid_y + ty * 2 + half]
            out_ref[slot // cap, (x % 4) // 2, slot % cap, pl.ds((x % 2) * 4, 4), :] = result[4 * half : 4 * half + 4]

    operate(q1, False, finish_four)


def per_device(
    velocity, density, tile_home, footprints, source_cell, source_wave, receivers, observed,
    pressure_old, pressure_now, adjoint_next, adjoint_now,
):
    owners = lax.axis_size("own")
    cores = lax.axis_size("shot")
    me = lax.axis_index("own")
    my_core = lax.axis_index("shot")
    held = velocity.shape[0]
    members, foot = footprints.shape[2:]
    cap = foot // owners
    nx, ny, nz = pressure_now.shape[-3:]
    home = jnp.take(tile_home, footprints, axis=0)
    slots = jnp.sum((home[..., None, :] < home[..., :, None]).astype(jnp.int32), axis=-1)
    wanted = me * cap + jnp.arange(cap, dtype=jnp.int32)
    row_all = jnp.sum(
        jnp.where(slots[..., None, :] == wanted[:, None], home[..., None, :] - me * held, 0), axis=-1
    )
    row_all = row_all.transpose(2, 0, 1, 3)
    row_mine = lax.dynamic_index_in_dim(row_all, my_core, 2, keepdims=False)
    my_slots = lax.dynamic_index_in_dim(
        lax.dynamic_index_in_dim(slots, me, 0, keepdims=False), my_core, 0, keepdims=False
    )
    vmem = pl.BlockSpec(memory_space=pltpu.VMEM)
    smem = pl.BlockSpec(memory_space=pltpu.SMEM)
    outgoing = pl.pallas_call(
        gather_kernel,
        out_shape=[jax.ShapeDtypeStruct((owners, 2, cap, 16, nz), jnp.bfloat16)] * members,
        in_specs=[smem, vmem, vmem],
        out_specs=[vmem] * members,
    )(row_mine.reshape(-1), velocity.reshape(held, 16, nz), density.reshape(held, 16, nz))
    band = band_matrices(nz)
    plain = pltpu.VMEM((nx, ny, nz), jnp.float32)
    padded = pltpu.VMEM((nx, ny + 2 * YOFF, nz), jnp.float32)
    models = [lax.all_to_all(sent, "own", split_axis=0, concat_axis=0, tiled=True) for sent in outgoing]
    arrived = []
    for member in range(members):
        field = pl.BlockSpec((1, 1, 1, nx, ny, nz), lambda i, member=member: (0, 0, member, 0, 0, 0))
        ready = pl.pallas_call(
            shot_kernel,
            grid=(1,),
            out_shape=jax.ShapeDtypeStruct((owners, cores, cap, 8, nz), jnp.float32),
            in_specs=[smem] * 5 + [vmem, vmem] + [field] * 4,
            out_specs=vmem,
            scratch_shapes=[plain, plain, pltpu.VMEM((nx, ny + 8, nz), jnp.float32), plain, plain, plain, padded,
                            pltpu.VMEM((nx, 8, nz), jnp.float32), padded, padded, plain, plain, padded, padded],
            compiler_params=pltpu.CompilerParams(vmem_limit_bytes=48 * 1024 * 1024),
            cost_estimate=pl.CostEstimate(flops=100_000_000, bytes_accessed=3_000_000, transcendentals=0),
        )(
            my_slots[member],
            source_cell[0, 0, member].reshape(1),
            receivers[0, 0, member],
            source_wave[0, 0, member],
            observed[0, 0, member].reshape(-1),
            models[member], band, pressure_old, pressure_now, adjoint_next, adjoint_now,
        )
        arrived.append(
            lax.all_to_all(
                ready.reshape(owners * cores, cap, 8, nz), ("own", "shot"), split_axis=0, concat_axis=0, tiled=True
            )
        )
    gradient = pl.pallas_call(
        scatter_kernel,
        out_shape=jax.ShapeDtypeStruct((held, 8, nz), jnp.float32),
        in_specs=[smem] + [vmem] * members,
        out_specs=vmem,
    )(row_all.reshape(-1), *arrived)
    return gradient.reshape(held, 4 // cores, 4, nz)


def solution(mesh):
    whole = P(("grp", "own"), None, None, None)
    fields = P(("grp", "own"), "shot", None, None, None, None)
    in_specs = (
        whole, whole, P("grp"), P("grp", None, None, None),
        P(("grp", "own"), "shot", None),
        P(("grp", "own"), "shot", None, None),
        P(("grp", "own"), "shot", None, None),
        P(("grp", "own"), "shot", None, None, None),
        fields, fields, fields, fields,
    )
    return jax.shard_map(
        per_device, mesh=mesh, in_specs=in_specs,
        out_specs=P(("grp", "own"), "shot", None, None), check_vma=False,
    )
```

time: 186 us -> 102 us (0.55)
  other arithmetic: 72.4 us -> 1.71 us
  Pallas kernels: 0 us -> 33.9 us
  local copies, waits for them, and re-layouts: 42.8 us -> 15.8 us
  waiting for transfers between devices: 35.8 us -> 26.8 us
  starting transfers between devices: 28.5 us -> 23.3 us
  between operations: 4.65 us -> 0.12 us
    pallas_call x0 -> x4, Pallas kernels: none -> 33.9 us  [the longest x2 28.6 us: per_device(): pl.pallas_call(shot_kernel, grid=(1,), out_shape=jax.ShapeDtypeStruct((ow...]
    mul x10 -> x0, other arithmetic: 29.8 us -> none  [the longest x6 24.3 us: apply_operator(): flux_pad = pad_along(half_buoys[dimension] * gradient, dimension)]
    add x7 -> x1, other arithmetic: 23.4 us -> 0.01 us  [per_device(): wanted = me * cap + jnp.arange(cap, dtype=jnp.int32)]
    gather x18 -> x2, local copies, waits for them, and re-layouts: 24.3 us -> 8.66 us  [per_device(): home = jnp.take(tile_home, footprints, axis=0)]
    scatter-add x8 -> x0, other arithmetic: 12.5 us -> none  [inject(): wavefield.reshape(-1).at[cell_index].add(amounts).reshape(wavefield.shape)]
    all_to_all x6 -> x4, waiting for transfers between devices: 35.8 us -> 26.8 us  [the longest x2 13.6 us: per_device(): lax.all_to_all(ready.reshape(owners * cores, cap, 8, nz), ('own', 'shot')...]
    slice x15 -> x1, local copies, waits for them, and re-layouts: 6.23 us -> 0.65 us  [per_device(): source_cell[0, 0, member].reshape(1)]
    all_to_all x6 -> x4, starting transfers between devices: 28.5 us -> 23.3 us  [the longest x2 12.1 us: per_device(): lax.all_to_all(ready.reshape(owners * cores, cap, 8, nz), ('own', 'shot')...]
  transfers between devices with their start and end apart: 6 -> 4, of which waited for: 6 -> 2; matrix products, arithmetic and copies ran while one was open for 11% -> 1% of each run, Pallas kernels for 0% -> 28%
where the time goes in v1:
time: 102 us
  Pallas kernels  33.9 us (33%)
  waiting for transfers between devices  26.8 us (26%)
  starting transfers between devices  23.3 us (23%)
  local copies, waits for them, and re-layouts  15.8 us (15%)
  other arithmetic  1.71 us (2%)
    pallas_call x2, Pallas kernels, per_device(): pl.pallas_call(shot_kernel, grid=(1,), out_shape=jax.ShapeDtypeStruct((ow...  28.6 us
    all_to_all x2, waiting for transfers between devices, per_device(): lax.all_to_all(ready.reshape(owners * cores, cap, 8, nz), ('own', 'shot')...  13.6 us
    all_to_all x2, waiting for transfers between devices, per_device(): lax.all_to_all(sent, 'own', split_axis=0, concat_axis=0, tiled=True)  13.2 us
    all_to_all x2, starting transfers between devices, per_device(): lax.all_to_all(ready.reshape(owners * cores, cap, 8, nz), ('own', 'shot')...  12.1 us
    all_to_all x2, starting transfers between devices, per_device(): lax.all_to_all(sent, 'own', split_axis=0, concat_axis=0, tiled=True)  11.2 us
    gather x2, local copies, waits for them, and re-layouts, per_device(): home = jnp.take(tile_home, footprints, axis=0)  8.66 us
    unnamed x26, local copies, waits for them, and re-layouts  5 us
    pallas_call x1, Pallas kernels, per_device(): pl.pallas_call(scatter_kernel, out_shape=jax.ShapeDtypeStruct((held, 8, n...  2.81 us
  transfers between devices with their start and end apart: 4, of which 2 were waited for; matrix products, arithmetic and copies ran while one was open for 1% of the time, Pallas kernels for 28%

profile of v1, /device:TPU:0, one launch (start us, length us, event | category | flops | bytes accessed | tf_op | source)
XLA Modules:
  0.0 101.6 jit_solution(13293218796039699889)
XLA Ops:
  0.0 0.0 copy-start
  0.0 0.0 copy-start.8
  0.0 0.7 copy-done.8
  0.7 0.1 reshape.60
  0.8 0.0 copy-done
  0.8 8.6 %gather_fusion = s32[2048]{0:T(1024)S(1)} fusion(s32[1024]{0:T(1024)S(1)} %copy-done, s32[2048]{0:T(1024)S(1)} %broadcast_clamp_fusion), kind=kCustom, calls=%fused_computation | custom fusion | bytes 24576 | tf_op jit(solution)/shard_map/jit(_take)/gather | solution.py:252
  9.4 0.1 reshape.59
  9.5 0.9 convert_reduce_fusion
  10.5 0.7 select_reduce_fusion
  11.2 0.7 reshape.52.rows_ref
  11.9 0.0 copy-start.5
  11.9 2.5 %shard_map.127 = (bf16[8,2,8,16,128]{4,3,2,1,0:T(8,128)(2,1)}, bf16[8,2,8,16,128]{4,3,2,1,0:T(8,128)(2,1)}) custom-call(s32[128]{0:T(128)} %reshape.52.rows_ref, bf16[128,16,128]{2,1,0:T(8,128)(2,1)} %bitcast.30, bf16[128,16,128]{2,1,0:T(8,128)(2,1)} %bitcast.31), custom_call_target="tpu_custom_call" | custom-call | tf_op jit(solution)/shard_map/pallas_call | solution.py:265
  14.4 0.0 copy-start.3
  14.4 0.0 copy-start.4
  14.4 7.4 %all-to-all-start = ((bf16[8,2,8,16,128]{4,3,2,1,0:T(8,128)(2,1)}), bf16[8,2,8,16,128]{4,3,2,1,0:T(8,128)(2,1)S(1)}, u32[]{:S(2)}, u32[]{:S(2)}) async-start(bf16[8,2,8,16,128]{4,3,2,1,0:T(8,128)(2,1)} %get-tuple-element.7), calls=%async_computation | async-start | bytes 1048576 | tf_op jit(solution)/shard_map/all_to_all | solution.py:274
  21.8 0.0 copy-start.10
  21.8 0.6 copy-done.10
  22.5 0.6 fusion
  23.1 13.2 %all-to-all-done.tiles_ref = bf16[8,2,8,16,128]{4,3,2,1,0:T(8,128)(2,1)S(1)} async-done(((bf16[8,2,8,16,128]{4,3,2,1,0:T(8,128)(2,1)}), bf16[8,2,8,16,128]{4,3,2,1,0:T(8,128)(2,1)S(1)}, u32[]{:S(2)}, u32[]{:S(2)}) %all-to-all-start) | async-done | bytes 524320 | tf_op jit(solution)/shard_map/all_to_all | solution.py:274
  36.3 0.0 copy-start.1
  36.3 0.0 copy-start.2
  36.3 3.8 %all-to-all-start.2 = ((bf16[8,2,8,16,128]{4,3,2,1,0:T(8,128)(2,1)}), bf16[8,2,8,16,128]{4,3,2,1,0:T(8,128)(2,1)S(1)}, u32[]{:S(2)}, u32[]{:S(2)}) async-start(bf16[8,2,8,16,128]{4,3,2,1,0:T(8,128)(2,1)} %get-tuple-element.8), calls=%async_computation.2 | async-start | bytes 1048576 | tf_op jit(solution)/shard_map/all_to_all | solution.py:274
  40.1 0.0 copy-start.11
  40.1 0.7 copy-done.11
  40.8 0.0 copy-start.12
  40.8 0.7 copy-done.12
  41.4 0.0 copy-start.9
  41.5 0.7 copy-done.9
  42.1 0.0 copy-done.5
  42.1 0.0 copy-done.3
  42.1 0.0 copy-done.4
  42.1 0.0 copy-done.1
  42.2 0.0 copy-done.2
  42.2 14.3 %shard_map.128 = f32[8,2,8,8,128]{4,3,2,1,0:T(8,128)} custom-call(s32[64]{0:T(128)S(1)} %get-tuple-element.18.slots_ref, s32[1]{0:T(128)} %bitcast.2.source_ref, s32[128]{0:T(128)S(1)} %get-tuple-element.16.recv_cells, f32[2]{0:T(128)S(1)} %get-tuple-element.14.wave_ref, f32[256]{0:T(256)S(1)} %get-tuple-element.12.obs_ref, ...), custom_call_target="tpu_custom_call" | custom-call | flops 100000000 | bytes 3000000 | tf_op jit(solution)/shard_map/pallas_call | solution.py:278
  56.5 0.0 all-to-all-done.2.tiles_ref
  56.5 6.1 %all-to-all-start.1 = ((f32[16,8,8,128]{3,2,1,0:T(8,128)}), f32[16,8,8,128]{3,2,1,0:T(8,128)S(1)}, u32[]{:S(2)}, u32[]{:S(2)}) async-start(f32[16,8,8,128]{3,2,1,0:T(8,128)} %bitcast.9), calls=%async_computation.1 | async-start | bytes 1048576 | tf_op jit(solution)/shard_map/all_to_all | solution.py:297
  62.6 14.3 %shard_map.129 = f32[8,2,8,8,128]{4,3,2,1,0:T(8,128)} custom-call(s32[64]{0:T(128)S(1)} %get-tuple-element.17.slots_ref, s32[1]{0:T(128)} %bitcast.11.source_ref, s32[128]{0:T(128)S(1)} %get-tuple-element.15.recv_cells, f32[2]{0:T(128)S(1)} %get-tuple-element.13.wave_ref, f32[256]{0:T(256)S(1)} %get-tuple-element.11.obs_ref, ...), custom_call_target="tpu_custom_call" | custom-call | flops 100000000 | bytes 3000000 | tf_op jit(solution)/shard_map/pallas_call | solution.py:278
  76.9 0.0 all-to-all-done.1.refs_0_
  76.9 0.0 copy-start.6
  76.9 0.8 copy-done.6
  77.7 6.0 %all-to-all-start.3 = ((f32[16,8,8,128]{3,2,1,0:T(8,128)}), f32[16,8,8,128]{3,2,1,0:T(8,128)S(1)}, u32[]{:S(2)}, u32[]{:S(2)}) async-start(f32[16,8,8,128]{3,2,1,0:T(8,128)} %bitcast.15), calls=%async_computation.3 | async-start | bytes 1048576 | tf_op jit(solution)/shard_map/all_to_all | solution.py:297
  83.8 0.7 reshape.51.rows_ref
  84.4 13.6 %all-to-all-done.3.refs_1_ = f32[16,8,8,128]{3,2,1,0:T(8,128)S(1)} async-done(((f32[16,8,8,128]{3,2,1,0:T(8,128)}), f32[16,8,8,128]{3,2,1,0:T(8,128)S(1)}, u32[]{:S(2)}, u32[]{:S(2)}) %all-to-all-start.3) | async-done | bytes 524320 | tf_op jit(solution)/shard_map/all_to_all | solution.py:297
  98.0 0.0 copy-start.7
  98.0 0.8 copy-done.7
  98.8 2.8 %shard_map.130 = f32[128,8,128]{2,1,0:T(8,128)} custom-call(s32[256]{0:T(256)} %reshape.51.rows_ref, f32[16,8,8,128]{3,2,1,0:T(8,128)} %copy-done.6, f32[16,8,8,128]{3,2,1,0:T(8,128)} %copy-done.7), custom_call_target="tpu_custom_call" | custom-call | tf_op jit(solution)/shard_map/pallas_call | solution.py:301
  (12 shorter events, 0.1 us)
Async XLA Ops:
  0.0 0.8 copy-start
  0.0 0.7 copy-start.8
  11.9 30.2 %copy-start.5 = (bf16[2,256,128]{2,1,0:T(8,128)(2,1)S(1)}, bf16[2,256,128]{2,1,0:T(8,128)(2,1)}, u32[]{:S(2)}) copy-start(bf16[2,256,128]{2,1,0:T(8,128)(2,1)} %constant.66.clone.band_ref) | copy-start | bytes 393220
  14.4 27.8 %copy-start.3 = (bf16[1,1,2,32,32,128]{5,4,3,2,1,0:T(8,128)(2,1)S(1)}, bf16[1,1,2,32,32,128]{5,4,3,2,1,0:T(8,128)(2,1)}, u32[]{:S(2)}) copy-start(bf16[1,1,2,32,32,128]{5,4,3,2,1,0:T(8,128)(2,1)} %next_ref.3) | copy-start | bytes 1572868
  14.4 27.8 %copy-start.4 = (bf16[1,1,2,32,32,128]{5,4,3,2,1,0:T(8,128)(2,1)S(1)}, bf16[1,1,2,32,32,128]{5,4,3,2,1,0:T(8,128)(2,1)}, u32[]{:S(2)}) copy-start(bf16[1,1,2,32,32,128]{5,4,3,2,1,0:T(8,128)(2,1)} %adj_ref.3) | copy-start | bytes 1572868
  14.4 21.9 %all-to-all-start = ((bf16[8,2,8,16,128]{4,3,2,1,0:T(8,128)(2,1)}), bf16[8,2,8,16,128]{4,3,2,1,0:T(8,128)(2,1)S(1)}, u32[]{:S(2)}, u32[]{:S(2)}) async-start(bf16[8,2,8,16,128]{4,3,2,1,0:T(8,128)(2,1)} %get-tuple-element.7), calls=%async_computation | async-start | bytes 1048576 | tf_op jit(solution)/shard_map/all_to_all | solution.py:274
  21.8 0.7 copy-start.10
  36.3 5.8 %copy-start.1 = (bf16[1,1,2,32,32,128]{5,4,3,2,1,0:T(8,128)(2,1)S(1)}, bf16[1,1,2,32,32,128]{5,4,3,2,1,0:T(8,128)(2,1)}, u32[]{:S(2)}) copy-start(bf16[1,1,2,32,32,128]{5,4,3,2,1,0:T(8,128)(2,1)} %old_ref.3) | copy-start | bytes 1572868
  36.3 5.8 %copy-start.2 = (bf16[1,1,2,32,32,128]{5,4,3,2,1,0:T(8,128)(2,1)S(1)}, bf16[1,1,2,32,32,128]{5,4,3,2,1,0:T(8,128)(2,1)}, u32[]{:S(2)}) copy-start(bf16[1,1,2,32,32,128]{5,4,3,2,1,0:T(8,128)(2,1)} %now_ref.3) | copy-start | bytes 1572868
  36.3 20.2 %all-to-all-start.2 = ((bf16[8,2,8,16,128]{4,3,2,1,0:T(8,128)(2,1)}), bf16[8,2,8,16,128]{4,3,2,1,0:T(8,128)(2,1)S(1)}, u32[]{:S(2)}, u32[]{:S(2)}) async-start(bf16[8,2,8,16,128]{4,3,2,1,0:T(8,128)(2,1)} %get-tuple-element.8), calls=%async_computation.2 | async-start | bytes 1048576 | tf_op jit(solution)/shard_map/all_to_all | solution.py:274
  40.1 0.7 copy-start.11
  40.8 0.7 copy-start.12
  41.4 0.7 copy-start.9
  56.5 20.4 %all-to-all-start.1 = ((f32[16,8,8,128]{3,2,1,0:T(8,128)}), f32[16,8,8,128]{3,2,1,0:T(8,128)S(1)}, u32[]{:S(2)}, u32[]{:S(2)}) async-start(f32[16,8,8,128]{3,2,1,0:T(8,128)} %bitcast.9), calls=%async_computation.1 | async-start | bytes 1048576 | tf_op jit(solution)/shard_map/all_to_all | solution.py:297
  76.9 0.8 copy-start.6
  77.7 20.3 %all-to-all-start.3 = ((f32[16,8,8,128]{3,2,1,0:T(8,128)}), f32[16,8,8,128]{3,2,1,0:T(8,128)S(1)}, u32[]{:S(2)}, u32[]{:S(2)}) async-start(f32[16,8,8,128]{3,2,1,0:T(8,128)} %bitcast.15), calls=%async_computation.3 | async-start | bytes 1048576 | tf_op jit(solution)/shard_map/all_to_all | solution.py:297
  98.0 0.8 copy-start.7

commit v2 on v1

--- a/solution.py
+++ b/solution.py
@@ -62,6 +62,76 @@
         lax.fori_loop(0, sources, body, 0)
 
 
+def exchange_kernel(axes, sent, got, send_sems, recv_sems, local_sem):
+    sizes = [lax.axis_size(axis) for axis in axes]
+    peers = sent.shape[0]
+    me = lax.axis_index(axes[0])
+    for axis, size in zip(axes[1:], sizes[1:]):
+        me = me * size + lax.axis_index(axis)
+
+    def place(peer):
+        if len(axes) == 1:
+            return {axes[0]: peer}
+        return {axes[0]: peer // sizes[1], axes[1]: peer % sizes[1]}
+
+    barrier = pltpu.get_barrier_semaphore()
+
+    def greet(d, carry):
+        pl.semaphore_signal(barrier, inc=1, device_id=place((me + d) % peers), device_id_type=pl.DeviceIdType.MESH)
+        return carry
+
+    lax.fori_loop(1, peers, greet, 0)
+    local = pltpu.make_async_copy(sent.at[me], got.at[me], local_sem)
+    local.start()
+    pl.semaphore_wait(barrier, peers - 1)
+
+    def copy(d):
+        peer = (me + d) % peers
+        return pltpu.make_async_remote_copy(
+            src_ref=sent.at[peer], dst_ref=got.at[me],
+            send_sem=send_sems.at[d], recv_sem=recv_sems.at[d],
+            device_id=place(peer), device_id_type=pl.DeviceIdType.MESH,
+        )
+
+    def start(d, carry):
+        copy(d).start()
+        return carry
+
+    def wait(d, carry):
+        copy(d).wait()
+        return carry
+
+    lax.fori_loop(1, peers, start, 0)
+    lax.fori_loop(1, peers, wait, 0)
+    local.wait()
+
+
+def exchange(sent, axes, number):
+    vmem = pl.BlockSpec(memory_space=pltpu.VMEM)
+    return pl.pallas_call(
+        functools.partial(exchange_kernel, axes),
+        out_shape=jax.ShapeDtypeStruct(sent.shape, sent.dtype),
+        in_specs=[vmem], out_specs=vmem,
+        scratch_shapes=[pltpu.SemaphoreType.DMA((sent.shape[0],)), pltpu.SemaphoreType.DMA((sent.shape[0],)), pltpu.SemaphoreType.DMA],
+        compiler_params=pltpu.CompilerParams(collective_id=number, has_side_effects=True),
+    )(sent)
+
+
+def lookup(tile_home, footprints):
+    side = int(round(tile_home.shape[0] ** 0.5))
+    foot = int(round(footprints.shape[-1] ** 0.5))
+    first = footprints[..., 0].reshape(-1)
+    spot = jnp.arange(foot, dtype=jnp.int32)
+    along = jnp.arange(side, dtype=jnp.int32)
+    pick_x = ((first // side)[:, None] + spot)[..., None] == along
+    pick_y = ((first % side)[:, None] + spot)[..., None] == along
+    grid = tile_home.reshape(side, side).astype(jnp.float32)
+    lines = jnp.dot(pick_x.astype(jnp.float32).reshape(-1, side), grid, precision=lax.Precision.HIGHEST)
+    lines = lines.reshape(first.shape[0], foot, 1, side)
+    home = jnp.sum(jnp.where(pick_y[:, None], lines, 0.0), axis=-1)
+    return home.astype(jnp.int32).reshape(footprints.shape)
+
+
 def taps(at, low):
     total = None
     for m, ratio in enumerate(RATIOS, start=1):
@@ -200,9 +270,7 @@
     operate(third, False, finish_two)
     add_at(pad_u, YOFF, source_ref[0], wave_ref[1])
 
-    q1 = buoy_q1 = inject_zero
-
-    minus_q2 = hz_free = None
+    q1 = inject_zero
 
     def finish_three(x, ty, here, padded, value, total):
         q1[x, padded, :] = 2.0 * value - next_ref[0, 0, 0, x, here, :].astype(jnp.float32) + vel[x, here, :] * total
@@ -249,7 +317,7 @@
     members, foot = footprints.shape[2:]
     cap = foot // owners
     nx, ny, nz = pressure_now.shape[-3:]
-    home = jnp.take(tile_home, footprints, axis=0)
+    home = lookup(tile_home, footprints)
     slots = jnp.sum((home[..., None, :] < home[..., :, None]).astype(jnp.int32), axis=-1)
     wanted = me * cap + jnp.arange(cap, dtype=jnp.int32)
     row_all = jnp.sum(
@@ -271,7 +339,10 @@
     band = band_matrices(nz)
     plain = pltpu.VMEM((nx, ny, nz), jnp.float32)
     padded = pltpu.VMEM((nx, ny + 2 * YOFF, nz), jnp.float32)
-    models = [lax.all_to_all(sent, "own", split_axis=0, concat_axis=0, tiled=True) for sent in outgoing]
+    models = [exchange(outgoing[0], ("own",), 0)]
+    for sent in outgoing[1:]:
+        sent, models[0] = lax.optimization_barrier((sent, models[0]))
+        models.append(lax.all_to_all(sent, "own", split_axis=0, concat_axis=0, tiled=True))
     arrived = []
     for member in range(members):
         field = pl.BlockSpec((1, 1, 1, nx, ny, nz), lambda i, member=member: (0, 0, member, 0, 0, 0))
@@ -293,11 +364,11 @@
             observed[0, 0, member].reshape(-1),
             models[member], band, pressure_old, pressure_now, adjoint_next, adjoint_now,
         )
-        arrived.append(
-            lax.all_to_all(
-                ready.reshape(owners * cores, cap, 8, nz), ("own", "shot"), split_axis=0, concat_axis=0, tiled=True
-            )
-        )
+        ready = ready.reshape(owners * cores, cap, 8, nz)
+        if member < members - 1:
+            arrived.append(lax.all_to_all(ready, ("own", "shot"), split_axis=0, concat_axis=0, tiled=True))
+        else:
+            arrived.append(exchange(ready, ("own", "shot"), 1))
     gradient = pl.pallas_call(
         scatter_kernel,
         out_shape=jax.ShapeDtypeStruct((held, 8, nz), jnp.float32),

time: 102 us -> 92.2 us (0.904); the launches traced: 102 us -> 90.4 us
  Pallas kernels: 33.9 us -> 65.4 us
  waiting for transfers between devices: 26.8 us -> 0.01 us
  starting transfers between devices: 23.3 us -> 14.6 us
  local copies, waits for them, and re-layouts: 15.8 us -> 7.74 us
    pallas_call x0 -> x2, Pallas kernels: none -> 32.3 us  [exchange(): pl.pallas_call(functools.partial(exchange_kernel, axes), out_shape=jax.Sh...]
    all_to_all x2 -> x1, waiting for transfers between devices: 13.6 us -> 0.01 us  [per_device(): lax.all_to_all(ready, ('own', 'shot'), split_axis=0, concat_axis=0, tiled...]
    all_to_all x2 -> x1, waiting for transfers between devices: 13.2 us -> 0.01 us  [per_device(): lax.all_to_all(sent, 'own', split_axis=0, concat_axis=0, tiled=True)]
    gather x2 -> x0, local copies, waits for them, and re-layouts: 8.66 us -> none  [per_device(): home = jnp.take(tile_home, footprints, axis=0)]
    all_to_all x2 -> x1, starting transfers between devices: 12.1 us -> 6.1 us  [per_device(): lax.all_to_all(ready, ('own', 'shot'), split_axis=0, concat_axis=0, tiled...]
    all_to_all x2 -> x1, starting transfers between devices: 11.2 us -> 8.47 us  [per_device(): lax.all_to_all(sent, 'own', split_axis=0, concat_axis=0, tiled=True)]
    unnamed x26 -> x28, local copies, waits for them, and re-layouts: 5 us -> 4.97 us
  transfers between devices with their start and end apart: 4 -> 2, of which waited for: 2 -> 0; matrix products, arithmetic and copies ran while one was open for 1% -> 2% of each run, Pallas kernels for 28% -> 48%
where the time goes in v2:
time: 92.2 us; the launch traced here: 90.4 us
  Pallas kernels  65.4 us (71%)
  starting transfers between devices  14.6 us (16%)
  local copies, waits for them, and re-layouts  7.74 us (8%)
  other arithmetic  2.24 us (2%)
    pallas_call x2, Pallas kernels, exchange(): pl.pallas_call(functools.partial(exchange_kernel, axes), out_shape=jax.Sh...  32.3 us
    pallas_call x2, Pallas kernels, per_device(): pl.pallas_call(shot_kernel, grid=(1,), out_shape=jax.ShapeDtypeStruct((ow...  27.8 us
    all_to_all x1, starting transfers between devices, per_device(): lax.all_to_all(sent, 'own', split_axis=0, concat_axis=0, tiled=True)  8.47 us
    all_to_all x1, starting transfers between devices, per_device(): lax.all_to_all(ready, ('own', 'shot'), split_axis=0, concat_axis=0, tiled...  6.1 us
    unnamed x28, local copies, waits for them, and re-layouts  4.97 us
    pallas_call x1, Pallas kernels, per_device(): pl.pallas_call(scatter_kernel, out_shape=jax.ShapeDtypeStruct((held, 8, n...  2.81 us
    pallas_call x1, Pallas kernels, per_device(): pl.pallas_call(gather_kernel, out_shape=[jax.ShapeDtypeStruct((owners, 2,...  2.5 us
  transfers between devices with their start and end apart: 2, of which 0 were waited for; matrix products, arithmetic and copies ran while one was open for 2% of the time, Pallas kernels for 48%

profile of v2, /device:TPU:0, one launch (start us, length us, event | category | flops | bytes accessed | tf_op | source)
XLA Modules:
  0.0 90.4 jit_solution(13670316123402089024)
XLA Ops:
  0.0 0.0 copy-start.8
  0.0 0.0 copy-start.9
  0.0 0.7 copy-done.9
  0.7 0.0 copy-done.8
  0.7 0.4 slice_reduce_fusion
  1.1 0.1 reshape_squeeze.15
  1.2 0.1 reshape.183
  1.3 0.1 iota_add_fusion
  1.4 0.1 iota_compare_fusion.1
  1.5 0.3 fusion.1
  1.7 0.1 copy.17
  1.8 0.4 select_reduce_fusion
  2.2 0.1 convert_element_type.31
  2.3 0.9 %convert_reduce_fusion = s32[8,2,2,64]{3,2,1,0:T(2,128)S(1)} fusion(s32[8,2,2,64]{3,2,1,0:T(2,128)S(1)} %convert_element_type.31), kind=kLoop, calls=%fused_computation | loop fusion | flops 391168 | bytes 16384 | tf_op jit(solution)/shard_map/reduce_sum | solution.py:321
  3.3 0.7 select_reduce_fusion.1
  4.0 0.7 reshape.177.rows_ref
  4.7 0.0 copy-start.5
  4.7 0.0 copy-start.6
  4.7 2.5 %shard_map.127 = (bf16[8,2,8,16,128]{4,3,2,1,0:T(8,128)(2,1)}, bf16[8,2,8,16,128]{4,3,2,1,0:T(8,128)(2,1)}) custom-call(s32[128]{0:T(128)} %reshape.177.rows_ref, bf16[128,16,128]{2,1,0:T(8,128)(2,1)} %bitcast.35, bf16[128,16,128]{2,1,0:T(8,128)(2,1)} %bitcast.36), custom_call_target="tpu_custom_call" | custom-call | tf_op jit(solution)/shard_map/pallas_call | solution.py:333
  7.2 0.0 copy-start.3
  7.2 0.0 copy-start.4
  7.2 16.5 %shard_map.128.tiles_ref = bf16[8,2,8,16,128]{4,3,2,1,0:T(8,128)(2,1)} custom-call(bf16[8,2,8,16,128]{4,3,2,1,0:T(8,128)(2,1)} %get-tuple-element.10.sent), custom_call_target="tpu_custom_call" | custom-call | tf_op jit(solution)/shard_map/pallas_call | solution.py:111
  23.7 0.0 copy-start
  23.7 0.0 copy-start.2
  23.8 8.5 %all-to-all-start.1 = ((bf16[8,2,8,16,128]{4,3,2,1,0:T(8,128)(2,1)}), bf16[8,2,8,16,128]{4,3,2,1,0:T(8,128)(2,1)S(1)}, u32[]{:S(2)}, u32[]{:S(2)}) async-start(bf16[8,2,8,16,128]{4,3,2,1,0:T(8,128)(2,1)} %get-tuple-element.12), calls=%async_computation.1 | async-start | bytes 1048576 | tf_op jit(solution)/shard_map/all_to_all | solution.py:345
  32.2 0.0 copy-start.11
  32.2 0.6 copy-done.11
  32.9 0.7 fusion.4
  33.5 0.0 copy-start.12
  33.5 0.7 copy-done.12
  34.2 0.0 copy-start.13
  34.2 0.7 copy-done.13
  34.9 0.0 copy-start.10
  34.9 0.7 copy-done.10
  35.6 0.0 copy-done.5
  35.6 0.0 copy-done.6
  35.6 0.0 copy-done.3
  35.6 0.0 copy-done.4
  35.6 0.0 copy-done
  35.6 0.0 copy-done.2
  35.6 14.2 %shard_map.129 = f32[8,2,8,8,128]{4,3,2,1,0:T(8,128)} custom-call(s32[64]{0:T(128)S(1)} %get-tuple-element.20.slots_ref, s32[1]{0:T(128)} %bitcast.3.source_ref, s32[128]{0:T(128)S(1)} %get-tuple-element.18.recv_cells, f32[2]{0:T(128)S(1)} %get-tuple-element.16.wave_ref, f32[256]{0:T(256)S(1)} %get-tuple-element.14.obs_ref, ...), custom_call_target="tpu_custom_call" | custom-call | flops 100000000 | bytes 3000000 | tf_op jit(solution)/shard_map/pallas_call | solution.py:349
  49.8 0.0 all-to-all-done.1.tiles_ref
  49.8 6.1 %all-to-all-start = ((f32[16,8,8,128]{3,2,1,0:T(8,128)}), f32[16,8,8,128]{3,2,1,0:T(8,128)S(1)}, u32[]{:S(2)}, u32[]{:S(2)}) async-start(f32[16,8,8,128]{3,2,1,0:T(8,128)} %bitcast.10), calls=%async_computation | async-start | bytes 1048576 | tf_op jit(solution)/shard_map/all_to_all | solution.py:369
  56.0 0.7 reshape.176.rows_ref
  56.7 13.6 %shard_map.130 = f32[8,2,8,8,128]{4,3,2,1,0:T(8,128)S(1)} custom-call(s32[64]{0:T(128)S(1)} %get-tuple-element.19.slots_ref, s32[1]{0:T(128)} %bitcast.12.source_ref, s32[128]{0:T(128)S(1)} %get-tuple-element.17.recv_cells, f32[2]{0:T(128)S(1)} %get-tuple-element.15.wave_ref, f32[256]{0:T(256)S(1)} %get-tuple-element.13.obs_ref, ...), custom_call_target="tpu_custom_call" | custom-call | flops 100000000 | bytes 3000000 | tf_op jit(solution)/shard_map/pallas_call | solution.py:349
  70.2 0.0 copy-start.1
  70.3 0.8 copy-done.1
  71.0 15.7 %shard_map.131.refs_1_ = f32[16,8,8,128]{3,2,1,0:T(8,128)} custom-call(f32[16,8,8,128]{3,2,1,0:T(8,128)} %bitcast.34), custom_call_target="tpu_custom_call" | custom-call | tf_op jit(solution)/shard_map/pallas_call | solution.py:111
  86.8 0.0 all-to-all-done.refs_0_
  86.8 0.0 copy-start.7
  86.8 0.8 copy-done.7
  87.6 2.8 %shard_map.132 = f32[128,8,128]{2,1,0:T(8,128)} custom-call(s32[256]{0:T(256)} %reshape.176.rows_ref, f32[16,8,8,128]{3,2,1,0:T(8,128)} %copy-done.7, f32[16,8,8,128]{3,2,1,0:T(8,128)} %shard_map.131.refs_1_), custom_call_target="tpu_custom_call" | custom-call | tf_op jit(solution)/shard_map/pallas_call | solution.py:372
  (14 shorter events, 0.1 us)
Async XLA Ops:
  0.0 0.7 copy-start.8
  0.0 0.7 copy-start.9
  4.7 30.9 %copy-start.5 = (bf16[1,1,2,32,32,128]{5,4,3,2,1,0:T(8,128)(2,1)S(1)}, bf16[1,1,2,32,32,128]{5,4,3,2,1,0:T(8,128)(2,1)}, u32[]{:S(2)}) copy-start(bf16[1,1,2,32,32,128]{5,4,3,2,1,0:T(8,128)(2,1)} %adj_ref.3) | copy-start | bytes 1572868
  4.7 30.9 %copy-start.6 = (bf16[2,256,128]{2,1,0:T(8,128)(2,1)S(1)}, bf16[2,256,128]{2,1,0:T(8,128)(2,1)}, u32[]{:S(2)}) copy-start(bf16[2,256,128]{2,1,0:T(8,128)(2,1)} %constant.79.clone.band_ref) | copy-start | bytes 393220
  7.2 28.4 %copy-start.3 = (bf16[1,1,2,32,32,128]{5,4,3,2,1,0:T(8,128)(2,1)S(1)}, bf16[1,1,2,32,32,128]{5,4,3,2,1,0:T(8,128)(2,1)}, u32[]{:S(2)}) copy-start(bf16[1,1,2,32,32,128]{5,4,3,2,1,0:T(8,128)(2,1)} %now_ref.3) | copy-start | bytes 1572868
  7.2 28.4 %copy-start.4 = (bf16[1,1,2,32,32,128]{5,4,3,2,1,0:T(8,128)(2,1)S(1)}, bf16[1,1,2,32,32,128]{5,4,3,2,1,0:T(8,128)(2,1)}, u32[]{:S(2)}) copy-start(bf16[1,1,2,32,32,128]{5,4,3,2,1,0:T(8,128)(2,1)} %next_ref.3) | copy-start | bytes 1572868
  23.7 11.9 %copy-start = (bf16[8,2,8,16,128]{4,3,2,1,0:T(8,128)(2,1)S(1)}, bf16[8,2,8,16,128]{4,3,2,1,0:T(8,128)(2,1)}, u32[]{:S(2)}) copy-start(bf16[8,2,8,16,128]{4,3,2,1,0:T(8,128)(2,1)} %shard_map.128.tiles_ref) | copy-start | bytes 1572868
  23.7 11.9 %copy-start.2 = (bf16[1,1,2,32,32,128]{5,4,3,2,1,0:T(8,128)(2,1)S(1)}, bf16[1,1,2,32,32,128]{5,4,3,2,1,0:T(8,128)(2,1)}, u32[]{:S(2)}) copy-start(bf16[1,1,2,32,32,128]{5,4,3,2,1,0:T(8,128)(2,1)} %old_ref.3) | copy-start | bytes 1572868
  23.8 26.1 %all-to-all-start.1 = ((bf16[8,2,8,16,128]{4,3,2,1,0:T(8,128)(2,1)}), bf16[8,2,8,16,128]{4,3,2,1,0:T(8,128)(2,1)S(1)}, u32[]{:S(2)}, u32[]{:S(2)}) async-start(bf16[8,2,8,16,128]{4,3,2,1,0:T(8,128)(2,1)} %get-tuple-element.12), calls=%async_computation.1 | async-start | bytes 1048576 | tf_op jit(solution)/shard_map/all_to_all | solution.py:345
  32.2 0.7 copy-start.11
  33.5 0.7 copy-start.12
  34.2 0.7 copy-start.13
  34.9 0.7 copy-start.10
  49.8 36.9 %all-to-all-start = ((f32[16,8,8,128]{3,2,1,0:T(8,128)}), f32[16,8,8,128]{3,2,1,0:T(8,128)S(1)}, u32[]{:S(2)}, u32[]{:S(2)}) async-start(f32[16,8,8,128]{3,2,1,0:T(8,128)} %bitcast.10), calls=%async_computation | async-start | bytes 1048576 | tf_op jit(solution)/shard_map/all_to_all | solution.py:369
  70.2 0.8 copy-start.1
  86.8 0.8 copy-start.7

commit v3 on v2

--- a/solution.py
+++ b/solution.py
@@ -151,7 +151,7 @@
 
 
 def shot_kernel(
-    slots_ref, source_ref, recv_cells, wave_ref, obs_ref,
+    member, slots_all, source_all, cells_all, wave_all, obs_all,
     tiles_ref, band_ref, old_ref, now_ref, next_ref, adj_ref,
     out_ref,
     vel, rho, buoy, hx, hy, hz, fy, div_z, pad_u, pad_w, image_one, image_two, third, inject_zero,
@@ -165,7 +165,7 @@
 
     def place(kx, carry):
         for ky in range(grid_y):
-            slot = slots_ref[kx * grid_y + ky]
+            slot = slots_all[member, kx * grid_y + ky]
             for which, field in ((0, vel), (1, rho)):
                 tile = tiles_ref[slot // cap, which, slot % cap].astype(jnp.float32)
                 for i in range(4):
@@ -261,14 +261,14 @@
     third[:, pl.ds(0, YOFF), :] = zero_edge
     third[:, pl.ds(YOFF + ny, YOFF), :] = zero_edge
     operate(pad_u, True, finish_one)
-    add_at(third, YOFF, source_ref[0], wave_ref[0])
+    add_at(third, YOFF, source_all[0, 0, member], wave_all[0, 0, member, 0])
 
     def finish_two(x, ty, here, padded, value, total):
         image_two[x, here, :] = total
         pad_u[x, padded, :] = 2.0 * value - pad_u[x, padded, :] + vel[x, here, :] * total
 
     operate(third, False, finish_two)
-    add_at(pad_u, YOFF, source_ref[0], wave_ref[1])
+    add_at(pad_u, YOFF, source_all[0, 0, member], wave_all[0, 0, member, 1])
 
     q1 = inject_zero
 
@@ -279,18 +279,18 @@
     q1[:, pl.ds(YOFF + ny, YOFF), :] = zero_edge
     operate(second, True, finish_three)
 
-    count = recv_cells.shape[0]
+    count = cells_all.shape[-1]
 
     def receive(step, carry):
         for sub in range(8):
             n = step * 8 + sub
-            cell = recv_cells[n]
+            cell = cells_all[0, 0, member, n]
             row, z = cell // nz, cell % nz
             x, y = row // ny, row % ny + YOFF
             spot = pl.ds(y, 1)
             pick = lane == z
-            q1[x, spot, :] += jnp.where(pick, pad_u[x, spot, :] - obs_ref[count + n], 0.0)
-            second[x, spot, :] -= jnp.where(pick, third[x, spot, :] - obs_ref[n], 0.0)
+            q1[x, spot, :] += jnp.where(pick, pad_u[x, spot, :] - obs_all[0, 0, member, 1, n], 0.0)
+            second[x, spot, :] -= jnp.where(pick, third[x, spot, :] - obs_all[0, 0, member, 0, n], 0.0)
         return carry
 
     lax.fori_loop(0, count // 8, receive, 0)
@@ -299,7 +299,7 @@
         q0 = 2.0 * value - second[x, padded, :] + vel[x, here, :] * total
         result = rho[x, here, :] * (value * image_two[x, here, :] + q0 * image_one[x, here, :])
         for half in range(2):
-            slot = slots_ref[(x // 4) * grid_y + ty * 2 + half]
+            slot = slots_all[member, (x // 4) * grid_y + ty * 2 + half]
             out_ref[slot // cap, (x % 4) // 2, slot % cap, pl.ds((x % 2) * 4, 4), :] = result[4 * half : 4 * half + 4]
 
     operate(q1, False, finish_four)
@@ -347,7 +347,7 @@
     for member in range(members):
         field = pl.BlockSpec((1, 1, 1, nx, ny, nz), lambda i, member=member: (0, 0, member, 0, 0, 0))
         ready = pl.pallas_call(
-            shot_kernel,
+            functools.partial(shot_kernel, member),
             grid=(1,),
             out_shape=jax.ShapeDtypeStruct((owners, cores, cap, 8, nz), jnp.float32),
             in_specs=[smem] * 5 + [vmem, vmem] + [field] * 4,
@@ -357,11 +357,7 @@
             compiler_params=pltpu.CompilerParams(vmem_limit_bytes=48 * 1024 * 1024),
             cost_estimate=pl.CostEstimate(flops=100_000_000, bytes_accessed=3_000_000, transcendentals=0),
         )(
-            my_slots[member],
-            source_cell[0, 0, member].reshape(1),
-            receivers[0, 0, member],
-            source_wave[0, 0, member],
-            observed[0, 0, member].reshape(-1),
+            my_slots, source_cell, receivers, source_wave, observed,
             models[member], band, pressure_old, pressure_now, adjoint_next, adjoint_now,
         )
         ready = ready.reshape(owners * cores, cap, 8, nz)

time: 92.2 us -> 90 us (0.976)
  the two profiles are of different devices: /device:TPU:0 before, /device:TPU:13 now
where the time goes in v3:
time: 90 us; the launch traced here: 89.4 us
  Pallas kernels  68.4 us (76%)
  starting transfers between devices  12.2 us (14%)
  local copies, waits for them, and re-layouts  6.04 us (7%)
  other arithmetic  2.24 us (2%)
    pallas_call x2, Pallas kernels, exchange(): pl.pallas_call(functools.partial(exchange_kernel, axes), out_shape=jax.Sh...  35.9 us
    pallas_call x2, Pallas kernels, per_device(): pl.pallas_call(functools.partial(shot_kernel, member), grid=(1,), out_sha...  27.2 us
    all_to_all x1, starting transfers between devices, per_device(): lax.all_to_all(ready, ('own', 'shot'), split_axis=0, concat_axis=0, tiled...  8.01 us
    all_to_all x1, starting transfers between devices, per_device(): lax.all_to_all(sent, 'own', split_axis=0, concat_axis=0, tiled=True)  4.22 us
    unnamed x28, local copies, waits for them, and re-layouts  3.99 us
    pallas_call x1, Pallas kernels, per_device(): pl.pallas_call(scatter_kernel, out_shape=jax.ShapeDtypeStruct((held, 8, n...  2.81 us
    pallas_call x1, Pallas kernels, per_device(): pl.pallas_call(gather_kernel, out_shape=[jax.ShapeDtypeStruct((owners, 2,...  2.48 us
  transfers between devices with their start and end apart: 2, of which 0 were waited for; matrix products, arithmetic and copies ran while one was open for 1% of the time, Pallas kernels for 51%

profile of v3, /device:TPU:13, one launch (start us, length us, event | category | flops | bytes accessed | tf_op | source)
XLA Modules:
  0.0 89.4 jit_solution(14711220036321522555)
XLA Ops:
  0.0 0.0 copy-start.12
  0.0 0.0 copy-start.13
  0.0 0.7 copy-done.13
  0.7 0.0 copy-done.12
  0.7 0.4 slice_reduce_fusion
  1.1 0.1 reshape_squeeze.3
  1.2 0.1 reshape.179
  1.3 0.1 iota_add_fusion
  1.4 0.1 iota_compare_fusion.1
  1.5 0.3 fusion.1
  1.7 0.1 copy.17
  1.8 0.4 select_reduce_fusion
  2.2 0.1 convert_element_type.31
  2.3 0.9 %convert_reduce_fusion = s32[8,2,2,64]{3,2,1,0:T(2,128)S(1)} fusion(s32[8,2,2,64]{3,2,1,0:T(2,128)S(1)} %convert_element_type.31), kind=kLoop, calls=%fused_computation | loop fusion | flops 391168 | bytes 16384 | tf_op jit(solution)/shard_map/reduce_sum | solution.py:321
  3.3 0.7 select_reduce_fusion.1
  4.0 0.7 reshape.173.rows_ref
  4.7 0.0 copy-start.6
  4.7 2.5 %shard_map.127 = (bf16[8,2,8,16,128]{4,3,2,1,0:T(8,128)(2,1)}, bf16[8,2,8,16,128]{4,3,2,1,0:T(8,128)(2,1)}) custom-call(s32[128]{0:T(128)} %reshape.173.rows_ref, bf16[128,16,128]{2,1,0:T(8,128)(2,1)} %bitcast.19, bf16[128,16,128]{2,1,0:T(8,128)(2,1)} %bitcast.20), custom_call_target="tpu_custom_call" | custom-call | tf_op jit(solution)/shard_map/pallas_call | solution.py:333
  7.2 0.0 copy-start.2
  7.2 0.0 copy-start.3
  7.2 18.0 %shard_map.128.tiles_ref = bf16[8,2,8,16,128]{4,3,2,1,0:T(8,128)(2,1)} custom-call(bf16[8,2,8,16,128]{4,3,2,1,0:T(8,128)(2,1)} %get-tuple-element.10.sent), custom_call_target="tpu_custom_call" | custom-call | tf_op jit(solution)/shard_map/pallas_call | solution.py:111
  25.2 0.0 copy-start
  25.2 0.0 copy-start.1
  25.2 0.0 copy-start.9
  25.2 0.0 copy-start.10
  25.2 4.2 %all-to-all-start.1 = ((bf16[8,2,8,16,128]{4,3,2,1,0:T(8,128)(2,1)}), bf16[8,2,8,16,128]{4,3,2,1,0:T(8,128)(2,1)S(1)}, u32[]{:S(2)}, u32[]{:S(2)}) async-start(bf16[8,2,8,16,128]{4,3,2,1,0:T(8,128)(2,1)} %get-tuple-element.12), calls=%async_computation.1 | async-start | bytes 1048576 | tf_op jit(solution)/shard_map/all_to_all | solution.py:345
  29.4 0.0 copy-start.7
  29.4 0.0 copy-start.8
  29.4 0.0 copy-done.6
  29.4 0.0 copy-done.2
  29.5 0.0 copy-done.3
  29.5 0.0 copy-done
  29.5 0.0 copy-done.1
  29.5 0.0 copy-done.9
  29.5 0.0 copy-done.10
  29.5 0.6 copy-done.7
  30.1 0.0 copy-done.8
  30.1 0.0 copy-start.4
  30.1 1.0 %copy-done.4 = bf16[8,2,8,16,128]{4,3,2,1,0:T(8,128)(2,1)S(1)} copy-done((bf16[8,2,8,16,128]{4,3,2,1,0:T(8,128)(2,1)S(1)}, bf16[8,2,8,16,128]{4,3,2,1,0:T(8,128)(2,1)}, u32[]{:S(2)}) %copy-start.4) | copy-done | bytes 524312
  31.2 13.8 %shard_map.129 = f32[8,2,8,8,128]{4,3,2,1,0:T(8,128)} custom-call(s32[2,64]{1,0:T(2,128)S(1)} %dynamic-slice_bitcast_fusion.1.slots_all, s32[1,1,2]{2,1,0:T(1,128)S(1)} %copy-done.10, s32[1,1,2,128]{3,2,1,0:T(2,128)S(1)} %copy-done.8, f32[1,1,2,2]{3,2,1,0:T(2,128)S(1)} %copy-done.9, f32[1,1,2,2,128]{4,3,2,1,0:T(2,128)S(1)} %copy-done.7, ...), custom_call_target="tpu_custom_call" | custom-call | flops 100000000 | bytes 3000000 | tf_op jit(solution)/shard_map/pallas_call | solution.py:349
  45.0 0.0 all-to-all-done.1.tiles_ref
  45.0 8.0 %all-to-all-start = ((f32[16,8,8,128]{3,2,1,0:T(8,128)}), f32[16,8,8,128]{3,2,1,0:T(8,128)S(1)}, u32[]{:S(2)}, u32[]{:S(2)}) async-start(f32[16,8,8,128]{3,2,1,0:T(8,128)} %bitcast.6), calls=%async_computation | async-start | bytes 1048576 | tf_op jit(solution)/shard_map/all_to_all | solution.py:365
  53.0 0.7 reshape.172.rows_ref
  53.7 13.4 %shard_map.130 = f32[8,2,8,8,128]{4,3,2,1,0:T(8,128)S(1)} custom-call(s32[2,64]{1,0:T(2,128)S(1)} %dynamic-slice_bitcast_fusion.1.slots_all, s32[1,1,2]{2,1,0:T(1,128)S(1)} %copy-done.10, s32[1,1,2,128]{3,2,1,0:T(2,128)S(1)} %copy-done.8, f32[1,1,2,2]{3,2,1,0:T(2,128)S(1)} %copy-done.9, f32[1,1,2,2,128]{4,3,2,1,0:T(2,128)S(1)} %copy-done.7, ...), custom_call_target="tpu_custom_call" | custom-call | flops 100000000 | bytes 3000000 | tf_op jit(solution)/shard_map/pallas_call | solution.py:349
  67.1 0.0 copy-start.5
  67.1 0.8 copy-done.5
  67.9 17.9 %shard_map.131.refs_1_ = f32[16,8,8,128]{3,2,1,0:T(8,128)} custom-call(f32[16,8,8,128]{3,2,1,0:T(8,128)} %bitcast.18), custom_call_target="tpu_custom_call" | custom-call | tf_op jit(solution)/shard_map/pallas_call | solution.py:111
  85.8 0.0 all-to-all-done.refs_0_
  85.8 0.0 copy-start.11
  85.8 0.8 copy-done.11
  86.6 2.8 %shard_map.132 = f32[128,8,128]{2,1,0:T(8,128)} custom-call(s32[256]{0:T(256)} %reshape.172.rows_ref, f32[16,8,8,128]{3,2,1,0:T(8,128)} %copy-done.11, f32[16,8,8,128]{3,2,1,0:T(8,128)} %shard_map.131.refs_1_), custom_call_target="tpu_custom_call" | custom-call | tf_op jit(solution)/shard_map/pallas_call | solution.py:368
  (10 shorter events, 0.1 us)
Async XLA Ops:
  0.0 0.7 copy-start.12
  0.0 0.7 copy-start.13
  4.7 24.8 %copy-start.6 = (bf16[2,256,128]{2,1,0:T(8,128)(2,1)S(1)}, bf16[2,256,128]{2,1,0:T(8,128)(2,1)}, u32[]{:S(2)}) copy-start(bf16[2,256,128]{2,1,0:T(8,128)(2,1)} %constant.79.clone.band_ref) | copy-start | bytes 393220
  7.2 22.3 %copy-start.2 = (bf16[1,1,2,32,32,128]{5,4,3,2,1,0:T(8,128)(2,1)S(1)}, bf16[1,1,2,32,32,128]{5,4,3,2,1,0:T(8,128)(2,1)}, u32[]{:S(2)}) copy-start(bf16[1,1,2,32,32,128]{5,4,3,2,1,0:T(8,128)(2,1)} %next_ref.3) | copy-start | bytes 1572868
  7.2 22.3 %copy-start.3 = (bf16[1,1,2,32,32,128]{5,4,3,2,1,0:T(8,128)(2,1)S(1)}, bf16[1,1,2,32,32,128]{5,4,3,2,1,0:T(8,128)(2,1)}, u32[]{:S(2)}) copy-start(bf16[1,1,2,32,32,128]{5,4,3,2,1,0:T(8,128)(2,1)} %adj_ref.3) | copy-start | bytes 1572868
  25.2 4.3 %copy-start = (bf16[1,1,2,32,32,128]{5,4,3,2,1,0:T(8,128)(2,1)S(1)}, bf16[1,1,2,32,32,128]{5,4,3,2,1,0:T(8,128)(2,1)}, u32[]{:S(2)}) copy-start(bf16[1,1,2,32,32,128]{5,4,3,2,1,0:T(8,128)(2,1)} %old_ref.3) | copy-start | bytes 1572868
  25.2 4.3 %copy-start.1 = (bf16[1,1,2,32,32,128]{5,4,3,2,1,0:T(8,128)(2,1)S(1)}, bf16[1,1,2,32,32,128]{5,4,3,2,1,0:T(8,128)(2,1)}, u32[]{:S(2)}) copy-start(bf16[1,1,2,32,32,128]{5,4,3,2,1,0:T(8,128)(2,1)} %now_ref.3) | copy-start | bytes 1572868
  25.2 4.3 %copy-start.9 = (f32[1,1,2,2]{3,2,1,0:T(2,128)S(1)}, f32[1,1,2,2]{3,2,1,0:T(2,128)}, u32[]{:S(2)}) copy-start(f32[1,1,2,2]{3,2,1,0:T(2,128)} %wave_all.3) | copy-start | bytes 52
  25.2 4.3 %copy-start.10 = (s32[1,1,2]{2,1,0:T(1,128)S(1)}, s32[1,1,2]{2,1,0:T(1,128)}, u32[]{:S(2)}) copy-start(s32[1,1,2]{2,1,0:T(1,128)} %source_all.3) | copy-start | bytes 28
  25.2 19.8 %all-to-all-start.1 = ((bf16[8,2,8,16,128]{4,3,2,1,0:T(8,128)(2,1)}), bf16[8,2,8,16,128]{4,3,2,1,0:T(8,128)(2,1)S(1)}, u32[]{:S(2)}, u32[]{:S(2)}) async-start(bf16[8,2,8,16,128]{4,3,2,1,0:T(8,128)(2,1)} %get-tuple-element.12), calls=%async_computation.1 | async-start | bytes 1048576 | tf_op jit(solution)/shard_map/all_to_all | solution.py:345
  29.4 0.7 copy-start.7
  29.4 0.7 copy-start.8
  30.1 1.0 %copy-start.4 = (bf16[8,2,8,16,128]{4,3,2,1,0:T(8,128)(2,1)S(1)}, bf16[8,2,8,16,128]{4,3,2,1,0:T(8,128)(2,1)}, u32[]{:S(2)}) copy-start(bf16[8,2,8,16,128]{4,3,2,1,0:T(8,128)(2,1)} %shard_map.128.tiles_ref) | copy-start | bytes 1572868
  45.0 40.8 %all-to-all-start = ((f32[16,8,8,128]{3,2,1,0:T(8,128)}), f32[16,8,8,128]{3,2,1,0:T(8,128)S(1)}, u32[]{:S(2)}, u32[]{:S(2)}) async-start(f32[16,8,8,128]{3,2,1,0:T(8,128)} %bitcast.6), calls=%async_computation | async-start | bytes 1048576 | tf_op jit(solution)/shard_map/all_to_all | solution.py:365
  67.1 0.8 copy-start.5
  85.8 0.8 copy-start.11
